TPU v7x, 32 devices: a whole 2x2x4 slice. The times are simulated.
32 devices in a mesh: group: 2 (over y), ctx: 8 (over z, x), tp: 2 (over core).
Axes of the slice: x: 2, y: 2, z: 4, core: 2. Of those that a mesh axis runs over, the one named last changes fastest.
Arguments:
- hidden: bfloat16 [256, 16384], P(('group', 'ctx')), parts along dimension 0, may hold values from -6 to 6
- q_base: bfloat16 [256, 8192], P(('group', 'ctx'), 'tp'), parts along dimension 0, may hold values from -6 to 6
- adapter_down: bfloat16 [16, 16384, 64], P(('group', 'ctx')), parts along dimension 0, may hold values from -0.046875 to 0.046875
- adapter_up: bfloat16 [16, 64, 8192], P(('group', 'ctx'), None, 'tp'), parts along dimension 0, may hold values from -0.75 to 0.75
- adapter_owner: int32 [2], P('group'), parts along dimension 0, may hold values from 0 to 7
- turn_start: int32 [2], P('group'), parts along dimension 0, may hold values from 512 to 2047
- shard_lengths: int32 [16], P('group'), parts along dimension 0, may hold values from 1 to 64, 384 in all
- stored_keys: bfloat16 [1024, 512], P(('group', 'ctx'), 'tp'), parts along dimension 0, may hold values from -250 to 250
- stored_values: bfloat16 [1024, 512], P(('group', 'ctx'), 'tp'), parts along dimension 0, may hold values from -6 to 6
- unrotated_turn_keys: bfloat16 [256, 512], P(('group', 'ctx'), 'tp'), parts along dimension 0, may hold values from -15 to 15
- incoming_values: bfloat16 [256, 512], P(('group', 'ctx'), 'tp'), parts along dimension 0, may hold values from -6 to 6
Outputs:
- attended: bfloat16 [256, 8192], P(('group', 'ctx'), 'tp'), parts along dimension 0
There are 2 independent parts, one for each index of `group`. A program takes and returns all parts, laid end to end along the dimension named above; each array names one. Nothing has to cross between parts.
Inputs may be any that keep to these rules, and one draw needn't show every extreme that they name: The used slots of shard s are its slots 0 .. shard_lengths[s] - 1; some shard uses all 64.
All inputs are finite; a program needn't handle non-finite values.
Results may differ from a plain program's by a relative error of at most 0.019.
The roundings to bfloat16 on the way count: a program that leaves them out, or rounds other values in their place, can miss the bound.
Values may be sent and summed in bfloat16 or wider, within the bound.
No kernel may reach another device: no remote copies, remote signals or barrier semaphores. Data moves between devices by JAX's collectives and lax.ppermute only.
A program may use at most 64 MiB of HBM per device.

v0:
```python
import math

import jax
import jax.numpy as jnp
from jax import lax
from jax.sharding import PartitionSpec as P

HEAD_SIZE = 128


def spread(shard, axis, root):
    mine = lax.axis_index(axis) == root
    return lax.psum(jnp.where(mine, shard, jnp.zeros_like(shard)), axis)


def apply_rotary(values, token_positions, heads):
    half_dim = HEAD_SIZE // 2
    inverse = jnp.exp(
        jnp.arange(half_dim, dtype=jnp.float32) * (-2.0 * math.log(500000.0) / HEAD_SIZE)
    )
    angles = token_positions.astype(jnp.float32)[:, None] * inverse[None, :]
    cosine = jnp.cos(angles)[:, None, :]
    sine = jnp.sin(angles)[:, None, :]
    shaped = values.reshape(values.shape[0], heads, HEAD_SIZE)
    first = shaped[..., :half_dim]
    second = shaped[..., half_dim:]
    turned = jnp.concatenate(
        [first * cosine - second * sine, second * cosine + first * sine], axis=-1
    )
    return turned.reshape(values.shape[0], heads * HEAD_SIZE)


def shards(
    hidden,
    q_base,
    adapter_down,
    adapter_up,
    adapter_owner,
    turn_start,
    shard_lengths,
    stored_keys,
    stored_values,
    unrotated_turn_keys,
    incoming_values,
):
    holder = adapter_owner[0]
    slot_down = adapter_down[0]
    slot_up = adapter_up[0]
    got_down, got_up = (spread(slot_down, "ctx", holder), spread(slot_up, "ctx", holder))
    lowrank = jnp.dot(hidden, got_down, preferred_element_type=jnp.float32).astype(jnp.bfloat16)
    adapter_delta = jnp.dot(lowrank, got_up, preferred_element_type=jnp.float32)
    token_count = q_base.shape[0]
    slot_count = stored_keys.shape[0]
    shard_rows = token_count + slot_count
    ctx_size = lax.axis_size("ctx")
    myself = lax.axis_index("ctx")
    query_heads = q_base.shape[1] // HEAD_SIZE
    kv_heads = unrotated_turn_keys.shape[1] // HEAD_SIZE
    groups = query_heads // kv_heads
    local_tokens = jnp.arange(token_count, dtype=jnp.int32)
    token_positions = turn_start[0] + myself * token_count + local_tokens
    query_rows = apply_rotary(
        q_base.astype(jnp.float32) + 0.5 * adapter_delta, token_positions, query_heads
    ).astype(jnp.bfloat16)
    rotated_turn_keys = apply_rotary(
        unrotated_turn_keys.astype(jnp.float32), token_positions, kv_heads
    ).astype(jnp.bfloat16)
    grouped = query_rows.reshape(token_count, kv_heads, groups, HEAD_SIZE)
    key_here = jnp.concatenate([stored_keys, rotated_turn_keys], axis=0)
    value_here = jnp.concatenate([stored_values, incoming_values], axis=0)
    mine = myself * token_count + local_tokens
    score_scale = 1.0 / math.sqrt(HEAD_SIZE)
    shard_ids = jnp.arange(ctx_size, dtype=jnp.int32)

    def absorb(state, key_block, value_block, start):
        highest, denominator, accum = state
        row_count = key_block.shape[0]
        global_rows = start + jnp.arange(row_count, dtype=jnp.int32)
        owner_shard = global_rows // shard_rows
        within = global_rows % shard_rows
        is_cache = within < slot_count
        lengths_here = jnp.sum(
            jnp.where(owner_shard[:, None] == shard_ids[None, :], shard_lengths[None, :], 0), axis=1
        )
        token_number = owner_shard * token_count + (within - slot_count)
        allowed = jnp.where(
            is_cache[None, :],
            (within < lengths_here)[None, :],
            token_number[None, :] <= mine[:, None],
        )
        allowed = allowed[:, None, None, :]
        key_head_rows = key_block.reshape(-1, kv_heads, HEAD_SIZE)
        value_head_rows = value_block.reshape(-1, kv_heads, HEAD_SIZE)
        scores = (
            jnp.einsum("rhgd,khd->rhgk", grouped, key_head_rows, preferred_element_type=jnp.float32)
            * score_scale
        )
        new_high = jnp.maximum(highest, jnp.max(jnp.where(allowed, scores, -1e30), axis=-1))
        weights = jnp.where(allowed, jnp.exp(scores - new_high[..., None]), 0.0)
        fade = jnp.exp(highest - new_high)
        denominator = denominator * fade + jnp.sum(weights, axis=-1)
        product = jnp.einsum(
            "rhgk,khd->rhgd",
            weights.astype(jnp.bfloat16),
            value_head_rows,
            preferred_element_type=jnp.float32,
        )
        accum = accum * fade[..., None] + product
        return (new_high, denominator, accum)

    initial = (
        jnp.full((token_count, kv_heads, groups), -1e30, jnp.float32),
        jnp.zeros((token_count, kv_heads, groups), jnp.float32),
        jnp.zeros((token_count, kv_heads, groups, HEAD_SIZE), jnp.float32),
    )
    block_rows = shard_rows * 8

    def fold_pieces(state, pieces, start):
        key_piece, value_piece = pieces
        row_count = key_piece.shape[0]
        if row_count > block_rows and row_count % block_rows == 0:
            count = row_count // block_rows
            key_split = key_piece.reshape(count, block_rows, key_piece.shape[1])
            value_split = value_piece.reshape(count, block_rows, value_piece.shape[1])

            def inner(carry, items):
                key_one, value_one, number = items
                return (absorb(carry, key_one, value_one, start + number * block_rows), None)

            numbers = jnp.arange(count, dtype=jnp.int32)
            state, unused = lax.scan(inner, state, (key_split, value_split, numbers))
            return state
        return absorb(state, key_piece, value_piece, start)

    state = fold_pieces(
        initial,
        (
            lax.all_gather(key_here, "ctx", axis=0, tiled=True),
            lax.all_gather(value_here, "ctx", axis=0, tiled=True),
        ),
        jnp.int32(0),
    )
    highest, denominator, accum = state
    attended = accum / denominator[..., None]
    return attended.reshape(token_count, query_heads * HEAD_SIZE).astype(jnp.bfloat16)


def solution(mesh):
    return jax.shard_map(
        shards,
        mesh=mesh,
        in_specs=(
            P(("group", "ctx"), None),
            P(("group", "ctx"), "tp"),
            P(("group", "ctx"), None, None),
            P(("group", "ctx"), None, "tp"),
            P("group"),
            P("group"),
            P("group"),
            P(("group", "ctx"), "tp"),
            P(("group", "ctx"), "tp"),
            P(("group", "ctx"), "tp"),
            P(("group", "ctx"), "tp"),
        ),
        out_specs=P(("group", "ctx"), "tp"),
        check_vma=False,
    )
```

profile of v0, /device:TPU:0, one launch (start us, length us, event | category | flops | bytes accessed | tf_op | source)
XLA Modules:
  0.0 146.3 jit_solution(9558791827877660342)
XLA Ops:
  6.5 0.0 copy-start
  7.3 1.5 select_bitcast_fusion
  8.7 0.8 select_bitcast_fusion.1
  9.6 0.0 all-reduce.3.cloned.1.call-update
  9.6 0.0 copy-start.7
  9.6 0.0 copy-start.2
  10.4 0.1 multiply_cosine_fusion
  10.5 0.1 subtract_convert_fusion.1
  10.6 0.1 pad_maximum_fusion.3
  10.7 35.0 %all_gather.6 = bf16[640,256]{1,0:T(8,128)(2,1)S(1)} all-gather(bf16[80,256]{1,0:T(8,128)(2,1)S(1)} %pad_maximum_fusion.1), channel_id=1, replica_groups=mesh['group'=2,'ctx'=8,'tp'=2] {'ctx'}, dimensions={0}, use_global_device_ids=true | all-gather | bytes 368640 | tf_op jit(solution)/shard_map/all_gather | solution.py:138
  45.7 0.2 copy.39
  45.9 31.5 %all_gather.7 = bf16[640,256]{1,0:T(8,128)(2,1)S(1)} all-gather(bf16[80,256]{1,0:T(8,128)(2,1)S(1)} %pad_maximum_fusion.2), channel_id=1, replica_groups=mesh['group'=2,'ctx'=8,'tp'=2] {'ctx'}, dimensions={0}, use_global_device_ids=true | all-gather | bytes 368640 | tf_op jit(solution)/shard_map/all_gather | solution.py:139
  77.5 0.2 copy.42
  77.7 0.1 select_reduce_fusion.1
  77.8 0.1 compare_select_fusion
  77.9 56.5 %all-reduce.3.cloned.1.call-done = (bf16[64,4096]{1,0:T(8,128)(2,1)}, bf16[16384,64]{0,1:T(8,128)(2,1)}) async-done(((bf16[64,4096]{1,0:T(8,128)(2,1)}, bf16[16384,64]{0,1:T(8,128)(2,1)}), (bf16[64,4096]{1,0:T(8,128)(2,1)}, bf16[16384,64]{0,1:T(8,128)(2,1)})) %all-reduce.3.cloned.1.call-update) | async-done | bytes 2621456 | tf_op jit(solution)/shard_map/psum | solution.py:13
  134.4 2.6 %fusion.2 = f32[2,8,32,128]{3,1,2,0:T(8,128)S(1)} fusion(bf16[64,4096]{1,0:T(8,128)(2,1)} %get-tuple-element.5, bf16[16384,64]{0,1:T(8,128)(2,1)} %get-tuple-element.6, bf16[16,16384]{1,0:T(8,128)(2,1)S(1)} %copy-done, bf16[16,4096]{1,0:T(8,128)(2,1)S(1)} %copy-done.2), kind=kOutput, calls=%fused_computation.7 | convolution fusion | flops 42140672 | bytes 3538944 | tf_op jit(solution)/shard_map/dot_general | solution.py:51
  137.1 0.1 copy.52
  137.1 0.1 subtract_convert_fusion
  137.3 0.1 pad_maximum_fusion
  137.4 0.4 select_reduce_fusion
  137.8 0.4 fusion.6
  138.3 0.4 fusion.5
  138.7 0.7 copy.60
  (27 shorter events, 0.1 us)
Async XLA Ops:
  6.5 127.9 %copy-start = (bf16[16,16384]{1,0:T(8,128)(2,1)S(1)}, bf16[16,16384]{1,0:T(8,128)(2,1)}, u32[]{:S(2)}) copy-start(bf16[16,16384]{1,0:T(8,128)(2,1)} %param.11) | copy-start | bytes 1572868
  6.5 127.9 %all-reduce.3.cloned.1.call-start = ((), (), s32[]{:S(2)}) async-start(), calls=%async_computation | async-start | bytes 5242880 | tf_op jit(solution)/shard_map/psum | solution.py:13
  7.3 1.5 %copy-start.1 = (bf16[1,64,4096]{2,1,0:T(8,128)(2,1)S(1)}, bf16[1,64,4096]{2,1,0:T(8,128)(2,1)}, u32[]{:S(2)}) copy-start(bf16[1,64,4096]{2,1,0:T(8,128)(2,1)} %param.14) | copy-start | bytes 1572868
  9.6 0.8 copy-start.5
  9.6 1.1 copy-start.3
  9.6 36.3 %copy-start.4 = (bf16[64,256]{1,0:T(8,128)(2,1)S(1)}, bf16[64,256]{1,0:T(8,128)(2,1)}, u32[]{:S(2)}) copy-start(bf16[64,256]{1,0:T(8,128)(2,1)} %param.19) | copy-start | bytes 98308
  9.6 36.3 %copy-start.6 = (bf16[16,256]{1,0:T(8,128)(2,1)S(1)}, bf16[16,256]{1,0:T(8,128)(2,1)}, u32[]{:S(2)}) copy-start(bf16[16,256]{1,0:T(8,128)(2,1)} %param.21) | copy-start | bytes 24580
  9.6 68.1 %copy-start.7 = (s32[8]{0:T(128)S(1)}, s32[8]{0:T(128)}, u32[]{:S(2)}) copy-start(s32[8]{0:T(128)} %param.17) | copy-start | bytes 100
  9.6 124.8 %copy-start.2 = (bf16[16,4096]{1,0:T(8,128)(2,1)S(1)}, bf16[16,4096]{1,0:T(8,128)(2,1)}, u32[]{:S(2)}) copy-start(bf16[16,4096]{1,0:T(8,128)(2,1)} %param.12) | copy-start | bytes 393220
Sparse Core Ops, SparseCore 0:
  11.1 123.2 all-reduce.2
where the time goes:
time: 146 us
  blocking collectives  66.5 us (46%)
  waiting for transfers between devices  56.5 us (39%)
  between operations  15 us (10%)
  matrix products  3.5 us (2%)
  other arithmetic  3.49 us (2%)
    psum x1, waiting for transfers between devices, spread(): return lax.psum(jnp.where(mine, shard, jnp.zeros_like(shard)), axis)  56.5 us
    all_gather x1, blocking collectives, shards(): lax.all_gather(key_here, 'ctx', axis=0, tiled=True)  35 us
    all_gather x1, blocking collectives, shards(): lax.all_gather(value_here, 'ctx', axis=0, tiled=True)  31.5 us
  transfers between devices with their start and end apart: 1, of which 1 were waited for; matrix products, arithmetic and copies ran while one was open for 1% of the time, Pallas kernels for 0%

commit v1 on v0

--- a/solution.py
+++ b/solution.py
@@ -1,11 +1,25 @@
+import functools
 import math
 
 import jax
 import jax.numpy as jnp
 from jax import lax
+from jax.experimental import pallas as pl
+from jax.experimental.pallas import tpu as pltpu
 from jax.sharding import PartitionSpec as P
 
+
 HEAD_SIZE = 128
+LANES = 128
+
+
+def rotary_tables(token_positions):
+    half_dim = HEAD_SIZE // 2
+    inverse = jnp.exp(
+        jnp.arange(half_dim, dtype=jnp.float32) * (-2.0 * math.log(500000.0) / HEAD_SIZE)
+    )
+    angles = token_positions.astype(jnp.float32)[:, None] * inverse[None, :]
+    return jnp.cos(angles), jnp.sin(angles)
 
 
 def spread(shard, axis, root):
@@ -15,12 +29,8 @@
 
 def apply_rotary(values, token_positions, heads):
     half_dim = HEAD_SIZE // 2
-    inverse = jnp.exp(
-        jnp.arange(half_dim, dtype=jnp.float32) * (-2.0 * math.log(500000.0) / HEAD_SIZE)
-    )
-    angles = token_positions.astype(jnp.float32)[:, None] * inverse[None, :]
-    cosine = jnp.cos(angles)[:, None, :]
-    sine = jnp.sin(angles)[:, None, :]
+    cosine, sine = rotary_tables(token_positions)
+    cosine, sine = cosine[:, None, :], sine[:, None, :]
     shaped = values.reshape(values.shape[0], heads, HEAD_SIZE)
     first = shaped[..., :half_dim]
     second = shaped[..., half_dim:]
@@ -30,7 +40,7 @@
     return turned.reshape(values.shape[0], heads * HEAD_SIZE)
 
 
-def shards(
+def shards_any(
     hidden,
     q_base,
     adapter_down,
@@ -44,9 +54,10 @@
     incoming_values,
 ):
     holder = adapter_owner[0]
-    slot_down = adapter_down[0]
-    slot_up = adapter_up[0]
-    got_down, got_up = (spread(slot_down, "ctx", holder), spread(slot_up, "ctx", holder))
+    got_down, got_up = (
+        spread(adapter_down[0], "ctx", holder),
+        spread(adapter_up[0], "ctx", holder),
+    )
     lowrank = jnp.dot(hidden, got_down, preferred_element_type=jnp.float32).astype(jnp.bfloat16)
     adapter_delta = jnp.dot(lowrank, got_up, preferred_element_type=jnp.float32)
     token_count = q_base.shape[0]
@@ -108,44 +119,467 @@
         accum = accum * fade[..., None] + product
         return (new_high, denominator, accum)
 
-    initial = (
+    state = (
         jnp.full((token_count, kv_heads, groups), -1e30, jnp.float32),
         jnp.zeros((token_count, kv_heads, groups), jnp.float32),
         jnp.zeros((token_count, kv_heads, groups, HEAD_SIZE), jnp.float32),
     )
     block_rows = shard_rows * 8
-
-    def fold_pieces(state, pieces, start):
-        key_piece, value_piece = pieces
-        row_count = key_piece.shape[0]
-        if row_count > block_rows and row_count % block_rows == 0:
-            count = row_count // block_rows
-            key_split = key_piece.reshape(count, block_rows, key_piece.shape[1])
-            value_split = value_piece.reshape(count, block_rows, value_piece.shape[1])
-
-            def inner(carry, items):
-                key_one, value_one, number = items
-                return (absorb(carry, key_one, value_one, start + number * block_rows), None)
-
-            numbers = jnp.arange(count, dtype=jnp.int32)
-            state, unused = lax.scan(inner, state, (key_split, value_split, numbers))
-            return state
-        return absorb(state, key_piece, value_piece, start)
-
-    state = fold_pieces(
-        initial,
-        (
-            lax.all_gather(key_here, "ctx", axis=0, tiled=True),
-            lax.all_gather(value_here, "ctx", axis=0, tiled=True),
-        ),
-        jnp.int32(0),
-    )
-    highest, denominator, accum = state
+    keys = lax.all_gather(key_here, "ctx", axis=0, tiled=True)
+    values = lax.all_gather(value_here, "ctx", axis=0, tiled=True)
+    row_count = keys.shape[0]
+    if row_count > block_rows and row_count % block_rows == 0:
+        count = row_count // block_rows
+        key_split = keys.reshape(count, block_rows, keys.shape[1])
+        value_split = values.reshape(count, block_rows, values.shape[1])
+
+        def inner(carry, items):
+            key_one, value_one, number = items
+            return (absorb(carry, key_one, value_one, number * block_rows), None)
+
+        numbers = jnp.arange(count, dtype=jnp.int32)
+        state, _ = lax.scan(inner, state, (key_split, value_split, numbers))
+    else:
+        state = absorb(state, keys, values, jnp.int32(0))
+    _, denominator, accum = state
     attended = accum / denominator[..., None]
     return attended.reshape(token_count, query_heads * HEAD_SIZE).astype(jnp.bfloat16)
 
 
+QUAD = 4
+
+
+def pack_kernel(cos_ref, sin_ref, sk_ref, sv_ref, tk_ref, tv_ref, kv_ref):
+    slots, width = sk_ref.shape
+    tokens = tk_ref.shape[0]
+    rows = slots + tokens
+    kv_ref[0:slots, :] = sk_ref[...]
+    kv_ref[rows : rows + slots, :] = sv_ref[...]
+    kv_ref[rows + slots : 2 * rows, :] = tv_ref[...]
+    cosine, sine = cos_ref[...], sin_ref[...]
+    for h in range(width // HEAD_SIZE):
+        at = slice(h * HEAD_SIZE, (h + 1) * HEAD_SIZE)
+        v = tk_ref[:, at].astype(jnp.float32)
+        turned = v * cosine + pltpu.roll(v, HEAD_SIZE // 2, 1) * sine
+        kv_ref[slots:rows, at] = turned.astype(kv_ref.dtype)
+
+
+def copy_all(jobs, sems):
+    for i, options in enumerate(jobs):
+        free = None
+        for condition, source, target in options:
+            if condition is None:
+                now = free
+            else:
+                now = condition if free is None else free & condition
+                free = ~condition if free is None else free & ~condition
+            copy = pltpu.make_async_copy(source, target, sems.at[i])
+            if now is None:
+                copy.start()
+            else:
+                pl.when(now)(copy.start)
+    for i, options in enumerate(jobs):
+        condition, source, target = options[-1]
+        pltpu.make_async_copy(source, target, sems.at[i]).wait()
+
+
+def down_at(pos_ref, down_ref, wide, half, other_z, other_x):
+    step = down_ref.shape[0] // 2
+    part = (pos_ref[0] * 2 + (pos_ref[1] ^ other_z)) * 2 + (pos_ref[2] ^ other_x)
+    at = pl.multiple_of(part * wide, LANES)
+    return down_ref.at[half * step : (half + 1) * step, pl.ds(at, wide)]
+
+
+def hidden_at(pos_ref, hidden_ref, wide, other_z, other_x):
+    part = (pos_ref[0] * 2 + (pos_ref[1] ^ other_z)) * 2 + (pos_ref[2] ^ other_x)
+    at = pl.multiple_of(part * wide, LANES)
+    return hidden_ref.at[:, pl.ds(at, wide)]
+
+
+def up_at(pos_ref, up_ref, half, piece, other_z, other_x):
+    step = up_ref.shape[0] // 4
+    columns = up_ref.shape[1] // QUAD
+    part = (pos_ref[1] ^ other_z) * 2 + (pos_ref[2] ^ other_x)
+    at = pl.multiple_of(part * columns, LANES)
+    row = (2 * half + piece) * step
+    return up_ref.at[row : row + step, pl.ds(at, columns)]
+
+
+def packed_down(ref, rank):
+    return ref.at[0 : rank // 2]
+
+
+def packed_up(ref, rank, piece):
+    columns = ref.shape[1] // 2
+    return ref.at[rank // 2 : rank // 2 + rank // 4, piece * columns : (piece + 1) * columns]
+
+
+def first_kernel(pos_ref, down_ref, up_ref, hidden_ref, sx_ref, sz_ref, hz_ref, sems):
+    rank = down_ref.shape[0]
+    wide = sx_ref.shape[2]
+    jobs = []
+    for j in range(2):
+        jobs.append([(None, hidden_at(pos_ref, hidden_ref, wide, 1, j), hz_ref.at[j])])
+    for half, ref in ((0, sx_ref), (1, sz_ref)):
+        for j in range(2):
+            oz, ox = (j, 1) if half == 0 else (1, j)
+            jobs.append(
+                [(None, down_at(pos_ref, down_ref, wide, half, oz, ox), packed_down(ref.at[j], rank))]
+            )
+            for piece in range(2):
+                jobs.append(
+                    [(None, up_at(pos_ref, up_ref, half, piece, oz, ox), packed_up(ref.at[j], rank, piece))]
+                )
+    copy_all(jobs, sems)
+
+
+def second_kernel(pos_ref, down_ref, up_ref, rx_ref, rz_ref, sz_ref, sx_ref, sems):
+    rank = down_ref.shape[0]
+    wide = sx_ref.shape[1]
+    z_differs, x_differs = pos_ref[3] == 1, pos_ref[4] == 1
+    jobs = []
+    for half, got, ref, oz, ox, differs in (
+        (0, rx_ref, sz_ref, 1, 0, x_differs),
+        (1, rz_ref, sx_ref, 0, 1, z_differs),
+    ):
+        jobs.append(
+            [
+                (differs, packed_down(got.at[1], rank), packed_down(ref, rank)),
+                (None, down_at(pos_ref, down_ref, wide, half, oz, ox), packed_down(ref, rank)),
+            ]
+        )
+        for piece in range(2):
+            target = packed_up(ref, rank, piece)
+            jobs.append(
+                [
+                    (differs, packed_up(got.at[1], rank, piece), target),
+                    (None, up_at(pos_ref, up_ref, half, piece, oz, ox), target),
+                ]
+            )
+    copy_all(jobs, sems)
+
+
+def hidden_kernel(pos_ref, hidden_ref, gz_ref, hx_ref, hf_ref, sems):
+    wide = hx_ref.shape[2]
+    copy_all(
+        [
+            [(None, hidden_at(pos_ref, hidden_ref, wide, 0, 1), hx_ref.at[0])],
+            [(None, hidden_at(pos_ref, hidden_ref, wide, 0, 0), hf_ref.at[0])],
+            [(None, gz_ref.at[1], hx_ref.at[1])],
+            [(None, gz_ref.at[0], hf_ref.at[1])],
+        ],
+        sems,
+    )
+
+
+def up_kernel(pos_ref, up_ref, rx_ref, rz_ref, r2z_ref, r2x_ref, out_ref, sems):
+    rank = up_ref.shape[0]
+    step = rank // 4
+    z_differs, x_differs = pos_ref[3] == 1, pos_ref[4] == 1
+    jobs = []
+    for half in range(2):
+        for piece in range(2):
+            row = (2 * half + piece) * step
+            target = out_ref.at[row : row + step]
+            late, early = (r2z_ref, rx_ref) if half == 0 else (r2x_ref, rz_ref)
+            one, two = (z_differs, x_differs) if half == 0 else (x_differs, z_differs)
+            jobs.append(
+                [
+                    (one, packed_up(late, rank, piece), target),
+                    (two, packed_up(early.at[0], rank, piece), target),
+                    (None, up_at(pos_ref, up_ref, half, piece, 0, 0), target),
+                ]
+            )
+    copy_all(jobs, sems)
+
+
+def lowrank_kernel(
+    far, pos_ref, down_ref, rx_ref, rz_ref, r2z_ref, r2x_ref, *refs
+):
+    count = 2 * far
+    hid = refs[:count]
+    keep_ref, send_ref, a_ref, h_ref, sems = refs[count:]
+    rank, wide = a_ref.shape
+    z_differs, x_differs = pos_ref[3] == 1, pos_ref[4] == 1
+    jobs = []
+    for half in range(2):
+        target = a_ref.at[half * (rank // 2) : (half + 1) * (rank // 2)]
+        late, early = (r2z_ref, rx_ref) if half == 0 else (r2x_ref, rz_ref)
+        one, two = (z_differs, x_differs) if half == 0 else (x_differs, z_differs)
+        jobs.append(
+            [
+                (one, packed_down(late, rank), target),
+                (two, packed_down(early.at[0], rank), target),
+                (None, down_at(pos_ref, down_ref, wide, half, 0, 0), target),
+            ]
+        )
+    tokens = hid[0].shape[1]
+    for i in range(count):
+        for j in range(2):
+            at = (2 * i + j) * tokens
+            h_ref[at : at + tokens, :] = hid[i][j]
+    copy_all(jobs, sems)
+    p = lax.dot_general(
+        h_ref[...], a_ref[...], (((1,), (1,)), ((), ())), preferred_element_type=jnp.float32
+    )
+    for i in range(count):
+        out = keep_ref if i < far else send_ref
+        for j in range(2):
+            at = (2 * i + j) * tokens
+            out[j, i % far] = p[at : at + tokens]
+
+
+def attend_kernel(far, slots, meta_ref, len_ref, *refs):
+    low = refs[:far]
+    ups = refs[far : far + QUAD]
+    kvs = refs[far + QUAD : far + QUAD + 3]
+    cos_ref, sin_ref, q_ref, o_ref, d_ref, qs_ref, k_ref, v_ref, low_ref = refs[far + QUAD + 3 :]
+    n = QUAD * far
+    tokens = q_ref.shape[0]
+    rows = kvs[0].shape[1] // 2
+    width = d_ref.shape[2]
+    query_heads = q_ref.shape[1] // HEAD_SIZE
+    kv_heads = k_ref.shape[1] // HEAD_SIZE
+    groups = query_heads // kv_heads
+    myself, pick = meta_ref[0], meta_ref[1]
+    for s in range(far):
+
+        @pl.when(pick == s)
+        def _(s=s):
+            low_ref[...] = low[s][...]
+
+    lowrank = low_ref[...].astype(jnp.bfloat16)
+    for i in range(QUAD):
+        d_ref[meta_ref[2 + i]] = jnp.dot(lowrank, ups[i][...], preferred_element_type=jnp.float32)
+    pieces = [kvs[0].at[s] for s in range(far)] + [kvs[1].at[s] for s in range(far)]
+    pieces += [kvs[2].at[s] for s in range(2 * far)]
+    for i, piece in enumerate(pieces):
+        k_ref[i * rows : (i + 1) * rows, :] = piece[0:rows, :]
+        v_ref[i * rows : (i + 1) * rows, :] = piece[rows : 2 * rows, :]
+    cosine, sine = cos_ref[...], sin_ref[...]
+    for h in range(query_heads):
+        b, off = divmod(h * HEAD_SIZE, width)
+        v = q_ref[:, h * HEAD_SIZE : (h + 1) * HEAD_SIZE].astype(jnp.float32)
+        v = v + 0.5 * d_ref[b, :, off : off + HEAD_SIZE]
+        turned = v * cosine + pltpu.roll(v, HEAD_SIZE // 2, 1) * sine
+        g = h % groups
+        qs_ref[h // groups, g * tokens : (g + 1) * tokens, :] = turned.astype(jnp.bfloat16)
+    shape = (tokens, n * rows)
+    col = lax.broadcasted_iota(jnp.int32, shape, 1)
+    token = myself * tokens + lax.broadcasted_iota(jnp.int32, shape, 0)
+    start = jnp.zeros(shape, jnp.int32)
+    limit = jnp.zeros(shape, jnp.int32)
+    first = jnp.zeros(shape, jnp.int32)
+    for i in range(n):
+        after = col >= i * rows
+        start = jnp.where(after, i * rows, start)
+        limit = jnp.where(after, len_ref[i], limit)
+        first = jnp.where(after, meta_ref[2 + QUAD + i] * tokens, first)
+    within = col - start
+    ok = jnp.where(within < slots, within - limit, within - slots + first - token - 1) < 0
+    bias = jnp.where(ok, 0.0, -1e30)[None]
+    scale = 1.0 / math.sqrt(HEAD_SIZE)
+    for kv in range(kv_heads):
+        at = slice(kv * HEAD_SIZE, (kv + 1) * HEAD_SIZE)
+        s = lax.dot_general(
+            qs_ref[kv], k_ref[:, at], (((1,), (1,)), ((), ())), preferred_element_type=jnp.float32
+        )
+        s = s.reshape(groups, tokens, n * rows) * scale + bias
+        w = jnp.exp(s - jnp.max(s, axis=-1, keepdims=True))
+        denominator = jnp.sum(w, axis=-1, keepdims=True)
+        w = w.reshape(groups * tokens, n * rows).astype(jnp.bfloat16)
+        o = jnp.dot(w, v_ref[:, at], preferred_element_type=jnp.float32)
+        o = o.reshape(groups, tokens, HEAD_SIZE) / denominator
+        for g in range(groups):
+            h = kv * groups + g
+            o_ref[:, h * HEAD_SIZE : (h + 1) * HEAD_SIZE] = o[g].astype(o_ref.dtype)
+
+
+def specs(space, count):
+    return [pl.BlockSpec(memory_space=space)] * count
+
+
+def call(kernel, shapes, inputs, outputs, scratch=()):
+    return pl.pallas_call(
+        kernel,
+        out_shape=[jax.ShapeDtypeStruct(s, d) for s, d in shapes],
+        in_specs=inputs,
+        out_specs=outputs,
+        scratch_shapes=list(scratch),
+    )
+
+
+def shards_quads(
+    hidden,
+    q_base,
+    adapter_down,
+    adapter_up,
+    adapter_owner,
+    turn_start,
+    shard_lengths,
+    stored_keys,
+    stored_values,
+    unrotated_turn_keys,
+    incoming_values,
+):
+    n = lax.axis_size("ctx")
+    tp_size = lax.axis_size("tp")
+    far = n // QUAD
+    myself = lax.axis_index("ctx")
+    core = lax.axis_index("tp")
+    quad, zl, x = myself // QUAD, myself // 2 % 2, myself % 2
+    owner = adapter_owner[0]
+    owner_quad, owner_zl, owner_x = owner // QUAD, owner // 2 % 2, owner % 2
+    tokens, features = hidden.shape
+    wide = features // (tp_size * QUAD)
+    rank = adapter_down.shape[2]
+    columns = adapter_up.shape[2]
+    quarter = columns // QUAD
+    slots, kv_width = stored_keys.shape
+    bf16, f32 = jnp.bfloat16, jnp.float32
+    smem, vmem, anywhere = pltpu.SMEM, pltpu.VMEM, pl.ANY
+
+    def permute(v, flip=0, shift=0, core_shift=0):
+        pairs = []
+        for a in range(n):
+            to = (a // QUAD + shift) % far * QUAD + (a % QUAD ^ flip)
+            for c in range(tp_size):
+                pairs.append((a * tp_size + c, to * tp_size + (c + core_shift) % tp_size))
+        return lax.ppermute(v, ("ctx", "tp"), pairs)
+
+    down, up = adapter_down[0].T, adapter_up[0]
+    pos = jnp.stack(
+        [
+            core,
+            zl,
+            x,
+            (zl != owner_zl).astype(jnp.int32),
+            (x != owner_x).astype(jnp.int32),
+        ]
+    )
+    packed = rank // 2 + rank // 4
+
+    sx, sz, hz = call(
+        first_kernel,
+        [((2, packed, wide), bf16), ((2, packed, wide), bf16), ((2, tokens, wide), bf16)],
+        specs(smem, 1) + specs(anywhere, 3),
+        specs(anywhere, 3),
+        [pltpu.SemaphoreType.DMA((14,))],
+    )(pos, down, up, hidden)
+    gz = permute(hz, 2)
+    rx = permute(sx, 1)
+    rz = permute(sz, 2)
+
+    hx, hf = call(
+        hidden_kernel,
+        [((2, tokens, wide), bf16), ((2, tokens, wide), bf16)],
+        specs(smem, 1) + specs(anywhere, 2),
+        specs(anywhere, 2),
+        [pltpu.SemaphoreType.DMA((4,))],
+    )(pos, hidden, gz)
+    hg = permute(hx, 1)
+    hid = [hf] + [permute(hf, 0, s) for s in range(1, far)]
+    hid += [hg] + [permute(hg, 0, s) for s in range(1, far)]
+
+    s2z, s2x = call(
+        second_kernel,
+        [((packed, wide), bf16), ((packed, wide), bf16)],
+        specs(smem, 1) + specs(anywhere, 4),
+        specs(anywhere, 2),
+        [pltpu.SemaphoreType.DMA((6,))],
+    )(pos, down, up, rx, rz)
+    r2z = permute(s2z, 2)
+    r2x = permute(s2x, 1)
+
+    (mine,) = call(
+        up_kernel,
+        [((rank, quarter), bf16)],
+        specs(smem, 1) + specs(anywhere, 5),
+        specs(anywhere, 1),
+        [pltpu.SemaphoreType.DMA((4,))],
+    )(pos, up, rx, rz, r2z, r2x)
+    quarters = mine
+    for s in range(1, far):
+        came = permute(mine, 0, s)
+        quarters = jnp.where((quad - owner_quad) % far == s, came, quarters)
+    up_z = permute(quarters, 2)
+    up_x = permute(quarters, 1)
+    up_zx = permute(up_z, 1)
+
+    partial_shape = ((2, far, tokens, rank), f32)
+    keep, send = call(
+        functools.partial(lowrank_kernel, far),
+        [partial_shape, partial_shape],
+        specs(smem, 1) + specs(anywhere, 5) + specs(vmem, 2 * far),
+        specs(vmem, 2),
+        [
+            pltpu.VMEM((rank, wide), bf16),
+            pltpu.VMEM((n * tokens, wide), bf16),
+            pltpu.SemaphoreType.DMA((2,)),
+        ],
+    )(pos, down, rx, rz, r2z, r2x, *hid)
+    total = keep
+    for c in range(tp_size):
+        total = total + permute(send, 1, 0, c)
+        if c:
+            total = total + permute(keep, 0, 0, c)
+    total = total[0] + permute(total[1], 2)
+    low = [total[0]] + [permute(total[s], 0, -s) for s in range(1, far)]
+
+    positions = turn_start[0] + myself * tokens + jnp.arange(tokens, dtype=jnp.int32)
+    cosine, sine = rotary_tables(positions)
+    cosine = jnp.concatenate([cosine, cosine], axis=1)
+    sine = jnp.concatenate([-sine, sine], axis=1)
+    kv_rows = 2 * (slots + tokens)
+    (kv,) = call(pack_kernel, [((kv_rows, kv_width), bf16)], specs(vmem, 6), specs(vmem, 1))(
+        cosine, sine, stored_keys, stored_values, unrotated_turn_keys, incoming_values
+    )
+    kv = jnp.stack([kv] + [permute(kv, 0, s) for s in range(1, far)])
+    kv_z = permute(kv, 2)
+    kv_x = permute(jnp.concatenate([kv, kv_z]), 1)
+
+    places = [(s, dz, dx) for dx in range(2) for dz in range(2) for s in range(far)]
+    ids = [((quad - s) % far * 2 + (zl ^ dz)) * 2 + (x ^ dx) for s, dz, dx in places]
+    blocks = [(zl ^ dz) * 2 + (x ^ dx) for dz, dx in ((0, 0), (1, 0), (0, 1), (1, 1))]
+    meta = jnp.stack([myself, (owner_quad - quad) % far] + blocks + ids)
+    lengths = shard_lengths[jnp.stack(ids)]
+    (out,) = call(
+        functools.partial(attend_kernel, far, slots),
+        [(q_base.shape, bf16)],
+        specs(smem, 2) + specs(vmem, far + QUAD + 6),
+        specs(vmem, 1),
+        [
+            pltpu.VMEM((QUAD, tokens, quarter), f32),
+            pltpu.VMEM((kv_width // HEAD_SIZE, columns // kv_width * tokens, HEAD_SIZE), bf16),
+            pltpu.VMEM((n * kv_rows // 2, kv_width), bf16),
+            pltpu.VMEM((n * kv_rows // 2, kv_width), bf16),
+            pltpu.VMEM((tokens, rank), f32),
+        ],
+    )(meta, lengths, *low, quarters, up_z, up_x, up_zx, kv, kv_z, kv_x, cosine, sine, q_base)
+    return out
+
+
+def fits_quads(mesh, hidden, q_base, adapter_down, stored_keys):
+    n, tp_size = mesh.shape["ctx"], mesh.shape["tp"]
+    if n % QUAD or n == QUAD:
+        return False
+    wide_whole = hidden.shape[1] % (tp_size * QUAD * LANES) == 0
+    quarter_whole = q_base.shape[1] % (QUAD * LANES) == 0
+    packs = adapter_down.shape[2] % 64 == 0 and hidden.shape[1] // tp_size == 2 * q_base.shape[1]
+    rows = n * (stored_keys.shape[0] + q_base.shape[0])
+    kv_width = stored_keys.shape[1]
+    queries = q_base.shape[1] // kv_width * q_base.shape[0]
+    room = rows * (8 * kv_width + 12 * queries)
+    return wide_whole and quarter_whole and packs and room < 16 * 2**20
+
+
 def solution(mesh):
+    def shards(*args):
+        hidden, q_base, adapter_down, stored_keys = args[0], args[1], args[2], args[7]
+        if fits_quads(mesh, hidden, q_base, adapter_down, stored_keys):
+            return shards_quads(*args)
+        return shards_any(*args)
+
     return jax.shard_map(
         shards,
         mesh=mesh,

time: 146 us -> 129 us (0.88)
  Pallas kernels: 0 us -> 66.8 us
  blocking collectives: 66.5 us -> 0 us
  waiting for transfers between devices: 56.5 us -> 26.5 us
  starting transfers between devices: 0.01 us -> 24.3 us
  between operations: 15 us -> 1.71 us
  local copies, waits for them, and re-layouts: 1.23 us -> 6.61 us
  matrix products: 3.5 us -> 0 us
    pallas_call x0 -> x7, Pallas kernels: none -> 66.8 us  [the longest x1 29.7 us: shards_quads(): call(first_kernel, [((2, packed, wide), bf16), ((2, packed, wide), bf16),...]
    all_gather x2 -> x0, blocking collectives: 66.5 us -> none  [the longest x1 35 us: shards(): lax.all_gather(key_here, 'ctx', axis=0, tiled=True)]
    psum x1 -> x0, waiting for transfers between devices: 56.5 us -> none  [spread(): return lax.psum(jnp.where(mine, shard, jnp.zeros_like(shard)), axis)]
    ppermute x0 -> x20, waiting for transfers between devices: none -> 26.5 us  [permute(): return lax.ppermute(v, ('ctx', 'tp'), pairs)]
    ppermute x0 -> x20, starting transfers between devices: none -> 24.3 us  [permute(): return lax.ppermute(v, ('ctx', 'tp'), pairs)]
    dot_general x3 -> x0, matrix products: 3.5 us -> none  [the longest x1 2.64 us: shards(): adapter_delta = jnp.dot(lowrank, got_up, preferred_element_type=jnp.float32)]
    unnamed x19 -> x38, local copies, waits for them, and re-layouts: 0.8 us -> 3.52 us
  transfers between devices with their start and end apart: 1 -> 20, of which waited for: 1 -> 6; matrix products, arithmetic and copies ran while one was open for 1% -> 4% of each run, Pallas kernels for 0% -> 26%
where the time goes in v1:
time: 129 us
  Pallas kernels  66.8 us (52%)
  waiting for transfers between devices  26.5 us (21%)
  starting transfers between devices  24.3 us (19%)
  local copies, waits for them, and re-layouts  6.61 us (5%)
  other arithmetic  2.69 us (2%)
  between operations  1.71 us (1%)
    pallas_call x1, Pallas kernels, shards_quads(): call(first_kernel, [((2, packed, wide), bf16), ((2, packed, wide), bf16),...  29.7 us
    ppermute x20, waiting for transfers between devices, permute(): return lax.ppermute(v, ('ctx', 'tp'), pairs)  26.5 us
    ppermute x20, starting transfers between devices, permute(): return lax.ppermute(v, ('ctx', 'tp'), pairs)  24.3 us
    pallas_call x1, Pallas kernels, shards_quads(): call(second_kernel, [((packed, wide), bf16), ((packed, wide), bf16)], spe...  13.7 us
    pallas_call x1, Pallas kernels, shards_quads(): call(hidden_kernel, [((2, tokens, wide), bf16), ((2, tokens, wide), bf16)...  9.74 us
    pallas_call x1, Pallas kernels, shards_quads(): call(up_kernel, [((rank, quarter), bf16)], specs(smem, 1) + specs(anywher...  5.78 us
    unnamed x38, local copies, waits for them, and re-layouts  3.52 us
    pallas_call x1, Pallas kernels, shards_quads(): call(functools.partial(attend_kernel, far, slots), [(q_base.shape, bf16)]...  3.35 us
  transfers between devices with their start and end apart: 20, of which 6 were waited for; matrix products, arithmetic and copies ran while one was open for 4% of the time, Pallas kernels for 26%

profile of v1, /device:TPU:0, one launch (start us, length us, event | category | flops | bytes accessed | tf_op | source)
XLA Modules:
  0.0 128.7 jit_solution(338823904046845865)
XLA Ops:
  1.3 29.7 %shard_map.109 = (bf16[2,48,2048]{2,1,0:T(8,128)(2,1)}, bf16[2,48,2048]{2,1,0:T(8,128)(2,1)}, bf16[2,16,2048]{2,1,0:T(8,128)(2,1)}) custom-call(s32[5]{0:T(128)} %stack.136.pos_ref, bf16[64,16384]{1,0:T(8,128)(2,1)} %bitcast.52, bf16[64,4096]{1,0:T(8,128)(2,1)} %bitcast.55, bf16[16,16384]{1,0:T(8,128)(2,1)} %hidden_ref.3), custom_call_target="tpu_custom_call" | custom-call | tf_op jit(solution)/shard_map/pallas_call | solution.py:462
  31.0 3.0 %collective-permute-start = (bf16[2,48,2048]{2,1,0:T(8,128)(2,1)}, bf16[2,48,2048]{2,1,0:T(8,128)(2,1)S(1)}, u32[]{:S(2)}, u32[]{:S(2)}) collective-permute-start(bf16[2,48,2048]{2,1,0:T(8,128)(2,1)} %get-tuple-element.14), channel_id=1, source_target_pairs={{0,2},{1,3},{2,0},{3,1},{4,6},{5,7},{6,4},{7,5},{8,10},{9,11},{10,... | collective-permute-start | bytes 1179656 | tf_op jit(solution)/shard_map/ppermute | solution.py:448
  34.0 1.6 %collective-permute-start.1 = (bf16[2,48,2048]{2,1,0:T(8,128)(2,1)}, bf16[2,48,2048]{2,1,0:T(8,128)(2,1)S(1)}, u32[]{:S(2)}, u32[]{:S(2)}) collective-permute-start(bf16[2,48,2048]{2,1,0:T(8,128)(2,1)} %get-tuple-element.15), channel_id=1, source_target_pairs={{0,4},{1,5},{2,6},{3,7},{4,0},{5,1},{6,2},{7,3},{8,12},{9,13},{10,... | collective-permute-start | bytes 1179656 | tf_op jit(solution)/shard_map/ppermute | solution.py:448
  37.5 1.5 %shard_map.114 = bf16[160,256]{1,0:T(8,128)(2,1)} custom-call(f32[16,128]{1,0:T(8,128)} %get-tuple-element.28.cos_ref.refs_9_, f32[16,128]{1,0:T(8,128)} %get-tuple-element.29.sin_ref.refs_10_, bf16[64,256]{1,0:T(8,128)(2,1)} %sk_ref.1, bf16[64,256]{1,0:T(8,128)(2,1)} %sv_ref.1, bf16[16,256]{1,0:T(8,128)(2,1)} %tk_ref.1, bf16[16,256]{1,0:T(8,128)(2,1)} %tv_ref.1), custom_call_target="tpu_custom_call" | custom-call | tf_op jit(solution)/shard_map/pallas_call | solution.py:534
  39.0 2.6 %collective-permute-start.17 = (bf16[160,256]{1,0:T(8,128)(2,1)}, bf16[160,256]{1,0:T(8,128)(2,1)S(1)}, u32[]{:S(2)}, u32[]{:S(2)}) collective-permute-start(bf16[160,256]{1,0:T(8,128)(2,1)} %shard_map.114), channel_id=1, source_target_pairs={{0,8},{1,9},{2,10},{3,11},{4,12},{5,13},{6,14},{7,15},{8,0},{9,1},... | collective-permute-start | bytes 245768 | tf_op jit(solution)/shard_map/ppermute | solution.py:448
  41.6 7.7 %collective-permute-done.4.gz_ref = bf16[2,16,2048]{2,1,0:T(8,128)(2,1)S(1)} collective-permute-done((bf16[2,16,2048]{2,1,0:T(8,128)(2,1)}, bf16[2,16,2048]{2,1,0:T(8,128)(2,1)S(1)}, u32[]{:S(2)}, u32[]{:S(2)}) %collective-permute-start.4) | collective-permute-done | bytes 131104 | tf_op jit(solution)/shard_map/ppermute | solution.py:448
  50.0 9.7 %shard_map.111 = (bf16[2,16,2048]{2,1,0:T(8,128)(2,1)}, bf16[2,16,2048]{2,1,0:T(8,128)(2,1)}) custom-call(s32[5]{0:T(128)} %stack.136.pos_ref, bf16[16,16384]{1,0:T(8,128)(2,1)} %hidden_ref.3, bf16[2,16,2048]{2,1,0:T(8,128)(2,1)} %copy-done.16), custom_call_target="tpu_custom_call" | custom-call | tf_op jit(solution)/shard_map/pallas_call | solution.py:473
  62.2 3.5 %collective-permute-start.5 = (bf16[2,16,2048]{2,1,0:T(8,128)(2,1)}, bf16[2,16,2048]{2,1,0:T(8,128)(2,1)S(1)}, u32[]{:S(2)}, u32[]{:S(2)}) collective-permute-start(bf16[2,16,2048]{2,1,0:T(8,128)(2,1)} %get-tuple-element.19.refs_0_), channel_id=1, source_target_pairs={{0,8},{1,9},{2,10},{3,11},{4,12},{5,13},{6,14},{7,15},{8,0},{9,1},... | collective-permute-start | bytes 393224 | tf_op jit(solution)/shard_map/ppermute | solution.py:448
  65.6 1.2 collective-permute-start.7
  68.3 13.7 %shard_map.110 = (bf16[48,2048]{1,0:T(8,128)(2,1)}, bf16[48,2048]{1,0:T(8,128)(2,1)}) custom-call(s32[5]{0:T(128)} %stack.136.pos_ref, bf16[64,16384]{1,0:T(8,128)(2,1)} %bitcast.53, bf16[64,4096]{1,0:T(8,128)(2,1)} %bitcast.56, bf16[2,48,2048]{2,1,0:T(8,128)(2,1)} %copy-done.1, bf16[2,48,2048]{2,1,0:T(8,128)(2,1)} %copy-done.2), custom_call_target="tpu_custom_call" | custom-call | tf_op jit(solution)/shard_map/pallas_call | solution.py:484
  82.1 2.4 %collective-permute-start.2 = (bf16[48,2048]{1,0:T(8,128)(2,1)}, bf16[48,2048]{1,0:T(8,128)(2,1)S(1)}, u32[]{:S(2)}, u32[]{:S(2)}) collective-permute-start(bf16[48,2048]{1,0:T(8,128)(2,1)} %get-tuple-element.16), channel_id=1, source_target_pairs={{0,4},{1,5},{2,6},{3,7},{4,0},{5,1},{6,2},{7,3},{8,12},{9,13},{10,... | collective-permute-start | bytes 589832 | tf_op jit(solution)/shard_map/ppermute | solution.py:448
  85.1 3.3 %collective-permute-done.2.r2z_ref = bf16[48,2048]{1,0:T(8,128)(2,1)S(1)} collective-permute-done((bf16[48,2048]{1,0:T(8,128)(2,1)}, bf16[48,2048]{1,0:T(8,128)(2,1)S(1)}, u32[]{:S(2)}, u32[]{:S(2)}) %collective-permute-start.2) | collective-permute-done | bytes 196640 | tf_op jit(solution)/shard_map/ppermute | solution.py:448
  88.4 2.0 %collective-permute-done.3.r2x_ref = bf16[48,2048]{1,0:T(8,128)(2,1)S(1)} collective-permute-done((bf16[48,2048]{1,0:T(8,128)(2,1)}, bf16[48,2048]{1,0:T(8,128)(2,1)S(1)}, u32[]{:S(2)}, u32[]{:S(2)}) %collective-permute-start.3) | collective-permute-done | bytes 196640 | tf_op jit(solution)/shard_map/ppermute | solution.py:448
  91.1 3.0 %shard_map.112 = (f32[2,2,16,64]{3,2,1,0:T(8,128)}, f32[2,2,16,64]{3,2,1,0:T(8,128)}) custom-call(s32[5]{0:T(128)} %stack.136.pos_ref, bf16[64,16384]{1,0:T(8,128)(2,1)} %bitcast.54, bf16[2,48,2048]{2,1,0:T(8,128)(2,1)} %copy-done.1, bf16[2,48,2048]{2,1,0:T(8,128)(2,1)} %copy-done.2, bf16[48,2048]{1,0:T(8,128)(2,1)} %copy-done.3, ...), custom_call_target="tpu_custom_call" | custom-call | tf_op jit(solution)/shard_map/pallas_call | solution.py:510
  94.8 1.3 collective-permute-start.10
  96.7 5.8 %shard_map.113 = bf16[64,1024]{1,0:T(8,128)(2,1)} custom-call(s32[5]{0:T(128)} %stack.136.pos_ref, bf16[64,4096]{1,0:T(8,128)(2,1)} %bitcast.57, bf16[2,48,2048]{2,1,0:T(8,128)(2,1)} %copy-done.1, bf16[2,48,2048]{2,1,0:T(8,128)(2,1)} %copy-done.2, bf16[48,2048]{1,0:T(8,128)(2,1)} %copy-done.3, bf16[48,2048]{1,0:T(8,128)(2,1)} %copy-done.4), custom_call_target="tpu_custom_call" | custom-call | tf_op jit(solution)/shard_map/pallas_call | solution.py:494
  103.6 1.4 %collective-permute-start.11 = (f32[2,16,64]{2,1,0:T(8,128)S(1)}, f32[2,16,64]{2,1,0:T(8,128)S(1)}, u32[]{:S(2)}, u32[]{:S(2)}) collective-permute-start(f32[2,16,64]{2,1,0:T(8,128)S(1)} %slice_bitcast_fusion), channel_id=1, source_target_pairs={{0,4},{1,5},{2,6},{3,7},{4,0},{5,1},{6,2},{7,3},{8,12},{9,13},{10,... | collective-permute-start | bytes 24584 | tf_op jit(solution)/shard_map/ppermute | solution.py:448
  105.0 6.8 %collective-permute-done.13 = bf16[64,1024]{1,0:T(8,128)(2,1)S(1)} collective-permute-done((bf16[64,1024]{1,0:T(8,128)(2,1)}, bf16[64,1024]{1,0:T(8,128)(2,1)S(1)}, u32[]{:S(2)}, u32[]{:S(2)}) %collective-permute-start.13) | collective-permute-done | bytes 131104 | tf_op jit(solution)/shard_map/ppermute | solution.py:448
  112.8 1.4 %collective-permute-start.15 = (bf16[64,1024]{1,0:T(8,128)(2,1)S(1)}, bf16[64,1024]{1,0:T(8,128)(2,1)S(1)}, u32[]{:S(2)}, u32[]{:S(2)}) collective-permute-start(bf16[64,1024]{1,0:T(8,128)(2,1)S(1)} %broadcast_select_fusion.refs_2_), channel_id=1, source_target_pairs={{0,2},{1,3},{2,0},{3,1},{4,6},{5,7},{6,4},{7,5},{8,10},{9,11},{10,... | collective-permute-start | bytes 393224 | tf_op jit(solution)/shard_map/ppermute | solution.py:448
  114.2 4.0 %collective-permute-done.14.refs_3_ = bf16[64,1024]{1,0:T(8,128)(2,1)S(1)} collective-permute-done((bf16[64,1024]{1,0:T(8,128)(2,1)S(1)}, bf16[64,1024]{1,0:T(8,128)(2,1)S(1)}, u32[]{:S(2)}, u32[]{:S(2)}) %collective-permute-start.14) | collective-permute-done | bytes 131104 | tf_op jit(solution)/shard_map/ppermute | solution.py:448
  118.2 1.3 collective-permute-start.16
  120.1 1.1 gather_fusion
  121.9 2.7 %collective-permute-done.12.refs_1_ = f32[16,64]{1,0:T(8,128)S(1)} collective-permute-done((f32[16,64]{1,0:T(8,128)S(1)}, f32[16,64]{1,0:T(8,128)S(1)}, u32[]{:S(2)}, u32[]{:S(2)}) %collective-permute-start.12) | collective-permute-done | bytes 4128 | tf_op jit(solution)/shard_map/ppermute | solution.py:448
  125.3 3.3 %shard_map.115 = bf16[16,4096]{1,0:T(8,128)(2,1)} custom-call(s32[14]{0:T(128)} %stack.119.meta_ref, s32[8]{0:T(128)} %gather_fusion, f32[16,64]{1,0:T(8,128)} %get-tuple-element.24.refs_0_, f32[16,64]{1,0:T(8,128)} %copy-done.18, bf16[64,1024]{1,0:T(8,128)(2,1)} %copy-done.8, bf16[64,1024]{1,0:T(8,128)(2,1)} %copy-done.11, bf16[64,1024]{1,0:T(8,128)(2,1)} %copy-done.12, ...), custom_call_target="tpu_custom_call" | custom-call | tf_op jit(solution)/shard_map/pallas_call | solution.py:546
  (78 shorter events, 12.9 us)
Async XLA Ops:
  0.0 120.1 %copy-start = (s32[8]{0:T(128)S(1)}, s32[8]{0:T(128)}, u32[]{:S(2)}) copy-start(s32[8]{0:T(128)} %param.17) | copy-start | bytes 100
  31.0 35.8 %collective-permute-start = (bf16[2,48,2048]{2,1,0:T(8,128)(2,1)}, bf16[2,48,2048]{2,1,0:T(8,128)(2,1)S(1)}, u32[]{:S(2)}, u32[]{:S(2)}) collective-permute-start(bf16[2,48,2048]{2,1,0:T(8,128)(2,1)} %get-tuple-element.14), channel_id=1, source_target_pairs={{0,2},{1,3},{2,0},{3,1},{4,6},{5,7},{6,4},{7,5},{8,10},{9,11},{10,... | collective-permute-start | bytes 1179656 | tf_op jit(solution)/shard_map/ppermute | solution.py:448
  34.0 32.8 %collective-permute-start.1 = (bf16[2,48,2048]{2,1,0:T(8,128)(2,1)}, bf16[2,48,2048]{2,1,0:T(8,128)(2,1)S(1)}, u32[]{:S(2)}, u32[]{:S(2)}) collective-permute-start(bf16[2,48,2048]{2,1,0:T(8,128)(2,1)} %get-tuple-element.15), channel_id=1, source_target_pairs={{0,4},{1,5},{2,6},{3,7},{4,0},{5,1},{6,2},{7,3},{8,12},{9,13},{10,... | collective-permute-start | bytes 1179656 | tf_op jit(solution)/shard_map/ppermute | solution.py:448
  35.6 13.8 %collective-permute-start.4 = (bf16[2,16,2048]{2,1,0:T(8,128)(2,1)}, bf16[2,16,2048]{2,1,0:T(8,128)(2,1)S(1)}, u32[]{:S(2)}, u32[]{:S(2)}) collective-permute-start(bf16[2,16,2048]{2,1,0:T(8,128)(2,1)} %get-tuple-element.18), channel_id=1, source_target_pairs={{0,4},{1,5},{2,6},{3,7},{4,0},{5,1},{6,2},{7,3},{8,12},{9,13},{10,... | collective-permute-start | bytes 393224 | tf_op jit(solution)/shard_map/ppermute | solution.py:448
  39.0 21.3 %collective-permute-start.17 = (bf16[160,256]{1,0:T(8,128)(2,1)}, bf16[160,256]{1,0:T(8,128)(2,1)S(1)}, u32[]{:S(2)}, u32[]{:S(2)}) collective-permute-start(bf16[160,256]{1,0:T(8,128)(2,1)} %shard_map.114), channel_id=1, source_target_pairs={{0,8},{1,9},{2,10},{3,11},{4,12},{5,13},{6,14},{7,15},{8,0},{9,1},... | collective-permute-start | bytes 245768 | tf_op jit(solution)/shard_map/ppermute | solution.py:448
  59.8 5.9 %collective-permute-start.6 = (bf16[2,16,2048]{2,1,0:T(8,128)(2,1)}, bf16[2,16,2048]{2,1,0:T(8,128)(2,1)S(1)}, u32[]{:S(2)}, u32[]{:S(2)}) collective-permute-start(bf16[2,16,2048]{2,1,0:T(8,128)(2,1)} %get-tuple-element.20), channel_id=1, source_target_pairs={{0,2},{1,3},{2,0},{3,1},{4,6},{5,7},{6,4},{7,5},{8,10},{9,11},{10,... | collective-permute-start | bytes 393224 | tf_op jit(solution)/shard_map/ppermute | solution.py:448
  61.2 63.4 %copy-start.7 = (bf16[2,160,256]{2,1,0:T(8,128)(2,1)}, bf16[2,160,256]{2,1,0:T(8,128)(2,1)S(1)}, u32[]{:S(2)}) copy-start(bf16[2,160,256]{2,1,0:T(8,128)(2,1)S(1)} %pad_maximum_fusion.1.refs_6_) | copy-start | bytes 491524
  61.2 34.8 %collective-permute-start.18 = (bf16[2,160,256]{2,1,0:T(8,128)(2,1)S(1)}, bf16[2,160,256]{2,1,0:T(8,128)(2,1)S(1)}, u32[]{:S(2)}, u32[]{:S(2)}) collective-permute-start(bf16[2,160,256]{2,1,0:T(8,128)(2,1)S(1)} %pad_maximum_fusion.1.refs_6_), channel_id=1, source_target_pairs={{0,4},{1,5},{2,6},{3,7},{4,0},{5,1},{6,2},{7,3},{8,12},{9,13},{10,... | collective-permute-start | bytes 491528 | tf_op jit(solution)/shard_map/ppermute | solution.py:448
  62.2 22.9 %collective-permute-start.5 = (bf16[2,16,2048]{2,1,0:T(8,128)(2,1)}, bf16[2,16,2048]{2,1,0:T(8,128)(2,1)S(1)}, u32[]{:S(2)}, u32[]{:S(2)}) collective-permute-start(bf16[2,16,2048]{2,1,0:T(8,128)(2,1)} %get-tuple-element.19.refs_0_), channel_id=1, source_target_pairs={{0,8},{1,9},{2,10},{3,11},{4,12},{5,13},{6,14},{7,15},{8,0},{9,1},... | collective-permute-start | bytes 393224 | tf_op jit(solution)/shard_map/ppermute | solution.py:448
  65.6 24.8 %copy-start.10 = (bf16[2,16,2048]{2,1,0:T(8,128)(2,1)}, bf16[2,16,2048]{2,1,0:T(8,128)(2,1)S(1)}, u32[]{:S(2)}) copy-start(bf16[2,16,2048]{2,1,0:T(8,128)(2,1)S(1)} %collective-permute-done.6.refs_2_) | copy-start | bytes 393220
  65.6 19.4 %collective-permute-start.7 = (bf16[2,16,2048]{2,1,0:T(8,128)(2,1)S(1)}, bf16[2,16,2048]{2,1,0:T(8,128)(2,1)S(1)}, u32[]{:S(2)}, u32[]{:S(2)}) collective-permute-start(bf16[2,16,2048]{2,1,0:T(8,128)(2,1)S(1)} %collective-permute-done.6.refs_2_), channel_id=1, source_target_pairs={{0,8},{1,9},{2,10},{3,11},{4,12},{5,13},{6,14},{7,15},{8,0},{9,1},... | collective-permute-start | bytes 393224 | tf_op jit(solution)/shard_map/ppermute | solution.py:448
  82.1 6.3 %collective-permute-start.2 = (bf16[48,2048]{1,0:T(8,128)(2,1)}, bf16[48,2048]{1,0:T(8,128)(2,1)S(1)}, u32[]{:S(2)}, u32[]{:S(2)}) collective-permute-start(bf16[48,2048]{1,0:T(8,128)(2,1)} %get-tuple-element.16), channel_id=1, source_target_pairs={{0,4},{1,5},{2,6},{3,7},{4,0},{5,1},{6,2},{7,3},{8,12},{9,13},{10,... | collective-permute-start | bytes 589832 | tf_op jit(solution)/shard_map/ppermute | solution.py:448
  84.5 5.9 %collective-permute-start.3 = (bf16[48,2048]{1,0:T(8,128)(2,1)}, bf16[48,2048]{1,0:T(8,128)(2,1)S(1)}, u32[]{:S(2)}, u32[]{:S(2)}) collective-permute-start(bf16[48,2048]{1,0:T(8,128)(2,1)} %get-tuple-element.17), channel_id=1, source_target_pairs={{0,2},{1,3},{2,0},{3,1},{4,6},{5,7},{6,4},{7,5},{8,10},{9,11},{10,... | collective-permute-start | bytes 589832 | tf_op jit(solution)/shard_map/ppermute | solution.py:448
  94.1 9.4 %collective-permute-start.9 = (f32[2,2,16,64]{3,2,1,0:T(8,128)}, f32[2,2,16,64]{3,2,1,0:T(8,128)S(1)}, u32[]{:S(2)}, u32[]{:S(2)}) collective-permute-start(f32[2,2,16,64]{3,2,1,0:T(8,128)} %get-tuple-element.22), channel_id=1, source_target_pairs={{0,3},{1,2},{2,1},{3,0},{4,7},{5,6},{6,5},{7,4},{8,11},{9,10},{10,... | collective-permute-start | bytes 49160 | tf_op jit(solution)/shard_map/ppermute | solution.py:448
  94.2 9.3 %collective-permute-start.8 = (f32[2,2,16,64]{3,2,1,0:T(8,128)}, f32[2,2,16,64]{3,2,1,0:T(8,128)S(1)}, u32[]{:S(2)}, u32[]{:S(2)}) collective-permute-start(f32[2,2,16,64]{3,2,1,0:T(8,128)} %get-tuple-element.22), channel_id=1, source_target_pairs={{0,2},{1,3},{2,0},{3,1},{4,6},{5,7},{6,4},{7,5},{8,10},{9,11},{10,... | collective-permute-start | bytes 49160 | tf_op jit(solution)/shard_map/ppermute | solution.py:448
  94.8 8.7 %collective-permute-start.10 = (f32[2,2,16,64]{3,2,1,0:T(8,128)}, f32[2,2,16,64]{3,2,1,0:T(8,128)S(1)}, u32[]{:S(2)}, u32[]{:S(2)}) collective-permute-start(f32[2,2,16,64]{3,2,1,0:T(8,128)} %get-tuple-element.21), channel_id=1, source_target_pairs={{0,1},{1,0},{2,3},{3,2},{4,5},{5,4},{6,7},{7,6},{8,9},{9,8},{10,11... | collective-permute-start | bytes 49160 | tf_op jit(solution)/shard_map/ppermute | solution.py:448
  96.1 28.6 %copy-start.6 = (bf16[2,160,256]{2,1,0:T(8,128)(2,1)}, bf16[2,160,256]{2,1,0:T(8,128)(2,1)S(1)}, u32[]{:S(2)}) copy-start(bf16[2,160,256]{2,1,0:T(8,128)(2,1)S(1)} %collective-permute-done.18.refs_7_) | copy-start | bytes 491524
  96.1 25.8 %collective-permute-start.19 = (bf16[4,160,256]{2,1,0:T(8,128)(2,1)S(1)}, bf16[4,160,256]{2,1,0:T(8,128)(2,1)S(1)}, u32[]{:S(2)}, u32[]{:S(2)}) collective-permute-start(bf16[4,160,256]{2,1,0:T(8,128)(2,1)S(1)} %pad_maximum_fusion), channel_id=1, source_target_pairs={{0,2},{1,3},{2,0},{3,1},{4,6},{5,7},{6,4},{7,5},{8,10},{9,11},{10,... | collective-permute-start | bytes 983048 | tf_op jit(solution)/shard_map/ppermute | solution.py:448
  102.5 9.3 %collective-permute-start.13 = (bf16[64,1024]{1,0:T(8,128)(2,1)}, bf16[64,1024]{1,0:T(8,128)(2,1)S(1)}, u32[]{:S(2)}, u32[]{:S(2)}) collective-permute-start(bf16[64,1024]{1,0:T(8,128)(2,1)} %shard_map.113), channel_id=1, source_target_pairs={{0,8},{1,9},{2,10},{3,11},{4,12},{5,13},{6,14},{7,15},{8,0},{9,1},... | collective-permute-start | bytes 393224 | tf_op jit(solution)/shard_map/ppermute | solution.py:448
  103.6 9.3 %collective-permute-start.11 = (f32[2,16,64]{2,1,0:T(8,128)S(1)}, f32[2,16,64]{2,1,0:T(8,128)S(1)}, u32[]{:S(2)}, u32[]{:S(2)}) collective-permute-start(f32[2,16,64]{2,1,0:T(8,128)S(1)} %slice_bitcast_fusion), channel_id=1, source_target_pairs={{0,4},{1,5},{2,6},{3,7},{4,0},{5,1},{6,2},{7,3},{8,12},{9,13},{10,... | collective-permute-start | bytes 24584 | tf_op jit(solution)/shard_map/ppermute | solution.py:448
  112.7 5.4 %collective-permute-start.14 = (bf16[64,1024]{1,0:T(8,128)(2,1)S(1)}, bf16[64,1024]{1,0:T(8,128)(2,1)S(1)}, u32[]{:S(2)}, u32[]{:S(2)}) collective-permute-start(bf16[64,1024]{1,0:T(8,128)(2,1)S(1)} %broadcast_select_fusion.refs_2_), channel_id=1, source_target_pairs={{0,4},{1,5},{2,6},{3,7},{4,0},{5,1},{6,2},{7,3},{8,12},{9,13},{10,... | collective-permute-start | bytes 393224 | tf_op jit(solution)/shard_map/ppermute | solution.py:448
  112.8 11.7 %collective-permute-start.15 = (bf16[64,1024]{1,0:T(8,128)(2,1)S(1)}, bf16[64,1024]{1,0:T(8,128)(2,1)S(1)}, u32[]{:S(2)}, u32[]{:S(2)}) collective-permute-start(bf16[64,1024]{1,0:T(8,128)(2,1)S(1)} %broadcast_select_fusion.refs_2_), channel_id=1, source_target_pairs={{0,2},{1,3},{2,0},{3,1},{4,6},{5,7},{6,4},{7,5},{8,10},{9,11},{10,... | collective-permute-start | bytes 393224 | tf_op jit(solution)/shard_map/ppermute | solution.py:448
  118.2 6.4 %collective-permute-start.16 = (bf16[64,1024]{1,0:T(8,128)(2,1)S(1)}, bf16[64,1024]{1,0:T(8,128)(2,1)S(1)}, u32[]{:S(2)}, u32[]{:S(2)}) collective-permute-start(bf16[64,1024]{1,0:T(8,128)(2,1)S(1)} %collective-permute-done.14.refs_3_), channel_id=1, source_target_pairs={{0,2},{1,3},{2,0},{3,1},{4,6},{5,7},{6,4},{7,5},{8,10},{9,11},{10,... | collective-permute-start | bytes 393224 | tf_op jit(solution)/shard_map/ppermute | solution.py:448
  120.0 4.5 %collective-permute-start.12 = (f32[16,64]{1,0:T(8,128)S(1)}, f32[16,64]{1,0:T(8,128)S(1)}, u32[]{:S(2)}, u32[]{:S(2)}) collective-permute-start(f32[16,64]{1,0:T(8,128)S(1)} %get-tuple-element.23), channel_id=1, source_target_pairs={{0,8},{1,9},{2,10},{3,11},{4,12},{5,13},{6,14},{7,15},{8,0},{9,1},... | collective-permute-start | bytes 12296 | tf_op jit(solution)/shard_map/ppermute | solution.py:448
  (15 other events, 62.0 us)

commit v2 on v1

--- a/solution.py
+++ b/solution.py
@@ -164,161 +164,148 @@
         kv_ref[slots:rows, at] = turned.astype(kv_ref.dtype)
 
 
-def copy_all(jobs, sems):
-    for i, options in enumerate(jobs):
-        free = None
-        for condition, source, target in options:
-            if condition is None:
-                now = free
-            else:
-                now = condition if free is None else free & condition
-                free = ~condition if free is None else free & ~condition
-            copy = pltpu.make_async_copy(source, target, sems.at[i])
-            if now is None:
-                copy.start()
-            else:
-                pl.when(now)(copy.start)
-    for i, options in enumerate(jobs):
-        condition, source, target = options[-1]
-        pltpu.make_async_copy(source, target, sems.at[i]).wait()
-
-
-def down_at(pos_ref, down_ref, wide, half, other_z, other_x):
-    step = down_ref.shape[0] // 2
-    part = (pos_ref[0] * 2 + (pos_ref[1] ^ other_z)) * 2 + (pos_ref[2] ^ other_x)
-    at = pl.multiple_of(part * wide, LANES)
-    return down_ref.at[half * step : (half + 1) * step, pl.ds(at, wide)]
-
-
-def hidden_at(pos_ref, hidden_ref, wide, other_z, other_x):
-    part = (pos_ref[0] * 2 + (pos_ref[1] ^ other_z)) * 2 + (pos_ref[2] ^ other_x)
-    at = pl.multiple_of(part * wide, LANES)
-    return hidden_ref.at[:, pl.ds(at, wide)]
-
-
-def up_at(pos_ref, up_ref, half, piece, other_z, other_x):
-    step = up_ref.shape[0] // 4
+def place():
+    myself = lax.axis_index("ctx")
+    return lax.axis_index("tp"), myself // QUAD, myself // 2 % 2, myself % 2
+
+
+def differs(owner_ref):
+    _, _, zl, x = place()
+    owner = owner_ref[0]
+    return owner // 2 % 2 != zl, owner % 2 != x
+
+
+def start_all(pairs, sems):
+    copies = [pltpu.make_async_copy(a, b, sems.at[i]) for i, (a, b) in enumerate(pairs)]
+    for copy in copies:
+        copy.start()
+    for copy in copies:
+        copy.wait()
+
+
+def feature_part(wide, other_z, other_x):
+    core, _, zl, x = place()
+    part = (core * 2 + (zl ^ other_z)) * 2 + (x ^ other_x)
+    return pl.ds(pl.multiple_of(part * wide, LANES), wide)
+
+
+def factor_pairs(down_ref, up_ref, target, half, other_z, other_x):
+    rank = down_ref.shape[0]
+    wide = target.shape[1]
     columns = up_ref.shape[1] // QUAD
-    part = (pos_ref[1] ^ other_z) * 2 + (pos_ref[2] ^ other_x)
-    at = pl.multiple_of(part * columns, LANES)
-    row = (2 * half + piece) * step
-    return up_ref.at[row : row + step, pl.ds(at, columns)]
-
-
-def packed_down(ref, rank):
-    return ref.at[0 : rank // 2]
-
-
-def packed_up(ref, rank, piece):
-    columns = ref.shape[1] // 2
-    return ref.at[rank // 2 : rank // 2 + rank // 4, piece * columns : (piece + 1) * columns]
-
-
-def first_kernel(pos_ref, down_ref, up_ref, hidden_ref, sx_ref, sz_ref, hz_ref, sems):
-    rank = down_ref.shape[0]
+    _, _, zl, x = place()
+    part = (zl ^ other_z) * 2 + (x ^ other_x)
+    at = pl.ds(pl.multiple_of(part * columns, LANES), columns)
+    top, step = rank // 2, rank // 4
+    pairs = [
+        (
+            down_ref.at[half * top : (half + 1) * top, feature_part(wide, other_z, other_x)],
+            target.at[0:top],
+        )
+    ]
+    for piece in range(2):
+        row = (2 * half + piece) * step
+        pairs.append(
+            (
+                up_ref.at[row : row + step, at],
+                target.at[top : top + step, piece * columns : (piece + 1) * columns],
+            )
+        )
+    return pairs
+
+
+def first_kernel(down_ref, up_ref, hidden_ref, sx_ref, sz_ref, hz_ref, sems):
     wide = sx_ref.shape[2]
-    jobs = []
+    pairs = []
     for j in range(2):
-        jobs.append([(None, hidden_at(pos_ref, hidden_ref, wide, 1, j), hz_ref.at[j])])
-    for half, ref in ((0, sx_ref), (1, sz_ref)):
-        for j in range(2):
-            oz, ox = (j, 1) if half == 0 else (1, j)
-            jobs.append(
-                [(None, down_at(pos_ref, down_ref, wide, half, oz, ox), packed_down(ref.at[j], rank))]
-            )
-            for piece in range(2):
-                jobs.append(
-                    [(None, up_at(pos_ref, up_ref, half, piece, oz, ox), packed_up(ref.at[j], rank, piece))]
-                )
-    copy_all(jobs, sems)
-
-
-def second_kernel(pos_ref, down_ref, up_ref, rx_ref, rz_ref, sz_ref, sx_ref, sems):
-    rank = down_ref.shape[0]
-    wide = sx_ref.shape[1]
-    z_differs, x_differs = pos_ref[3] == 1, pos_ref[4] == 1
-    jobs = []
-    for half, got, ref, oz, ox, differs in (
-        (0, rx_ref, sz_ref, 1, 0, x_differs),
-        (1, rz_ref, sx_ref, 0, 1, z_differs),
+        pairs.append((hidden_ref.at[:, feature_part(wide, 1, j)], hz_ref.at[j]))
+    for j in range(2):
+        pairs += factor_pairs(down_ref, up_ref, sx_ref.at[j], 0, j, 1)
+    for j in range(2):
+        pairs += factor_pairs(down_ref, up_ref, sz_ref.at[j], 1, 1, j)
+    start_all(pairs, sems)
+
+
+def own_kernel(down_ref, up_ref, hidden_ref, ox_ref, oz_ref, hh_ref, sems):
+    wide = ox_ref.shape[2]
+    pairs = []
+    for j in range(2):
+        pairs.append((hidden_ref.at[:, feature_part(wide, 0, j)], hh_ref.at[j]))
+    for j in range(2):
+        pairs += factor_pairs(down_ref, up_ref, ox_ref.at[j], 0, j, 0)
+    for j in range(2):
+        pairs += factor_pairs(down_ref, up_ref, oz_ref.at[j], 1, 0, j)
+    start_all(pairs, sems)
+
+
+def hidden_kernel(hh_ref, gz_ref, hx_ref, hf_ref):
+    hx_ref[0] = hh_ref[1]
+    hx_ref[1] = gz_ref[1]
+    hf_ref[0] = hh_ref[0]
+    hf_ref[1] = gz_ref[0]
+
+
+def second_kernel(owner_ref, ox_ref, oz_ref, rx_ref, rz_ref, sz_ref, sx_ref):
+    z_differs, x_differs = differs(owner_ref)
+
+    @pl.when(x_differs)
+    def _():
+        sz_ref[...] = rx_ref[1]
+
+    @pl.when(~x_differs)
+    def _():
+        sz_ref[...] = ox_ref[1]
+
+    @pl.when(z_differs)
+    def _():
+        sx_ref[...] = rz_ref[1]
+
+    @pl.when(~z_differs)
+    def _():
+        sx_ref[...] = oz_ref[1]
+
+
+def choose_late(owner_ref, ox_ref, oz_ref, rx_ref, rz_ref, r2z_ref, r2x_ref, put):
+    z_differs, x_differs = differs(owner_ref)
+    for half, late, early, own, one, two in (
+        (0, r2z_ref, rx_ref, ox_ref, z_differs, x_differs),
+        (1, r2x_ref, rz_ref, oz_ref, x_differs, z_differs),
     ):
-        jobs.append(
-            [
-                (differs, packed_down(got.at[1], rank), packed_down(ref, rank)),
-                (None, down_at(pos_ref, down_ref, wide, half, oz, ox), packed_down(ref, rank)),
-            ]
-        )
-        for piece in range(2):
-            target = packed_up(ref, rank, piece)
-            jobs.append(
-                [
-                    (differs, packed_up(got.at[1], rank, piece), target),
-                    (None, up_at(pos_ref, up_ref, half, piece, oz, ox), target),
-                ]
-            )
-    copy_all(jobs, sems)
-
-
-def hidden_kernel(pos_ref, hidden_ref, gz_ref, hx_ref, hf_ref, sems):
-    wide = hx_ref.shape[2]
-    copy_all(
-        [
-            [(None, hidden_at(pos_ref, hidden_ref, wide, 0, 1), hx_ref.at[0])],
-            [(None, hidden_at(pos_ref, hidden_ref, wide, 0, 0), hf_ref.at[0])],
-            [(None, gz_ref.at[1], hx_ref.at[1])],
-            [(None, gz_ref.at[0], hf_ref.at[1])],
-        ],
-        sems,
-    )
-
-
-def up_kernel(pos_ref, up_ref, rx_ref, rz_ref, r2z_ref, r2x_ref, out_ref, sems):
-    rank = up_ref.shape[0]
-    step = rank // 4
-    z_differs, x_differs = pos_ref[3] == 1, pos_ref[4] == 1
-    jobs = []
-    for half in range(2):
+        pl.when(one)(functools.partial(put, half, late))
+        pl.when(~one & two)(functools.partial(put, half, early.at[0]))
+        pl.when(~one & ~two)(functools.partial(put, half, own.at[0]))
+
+
+def up_kernel(owner_ref, *refs):
+    out_ref = refs[6]
+    rank, columns = out_ref.shape
+    top, step = rank // 2, rank // 4
+
+    def put(half, ref):
         for piece in range(2):
             row = (2 * half + piece) * step
-            target = out_ref.at[row : row + step]
-            late, early = (r2z_ref, rx_ref) if half == 0 else (r2x_ref, rz_ref)
-            one, two = (z_differs, x_differs) if half == 0 else (x_differs, z_differs)
-            jobs.append(
-                [
-                    (one, packed_up(late, rank, piece), target),
-                    (two, packed_up(early.at[0], rank, piece), target),
-                    (None, up_at(pos_ref, up_ref, half, piece, 0, 0), target),
-                ]
-            )
-    copy_all(jobs, sems)
-
-
-def lowrank_kernel(
-    far, pos_ref, down_ref, rx_ref, rz_ref, r2z_ref, r2x_ref, *refs
-):
+            out_ref[row : row + step, :] = ref[
+                top : top + step, piece * columns : (piece + 1) * columns
+            ]
+
+    choose_late(owner_ref, *refs[:6], put)
+
+
+def lowrank_kernel(far, owner_ref, *refs):
     count = 2 * far
-    hid = refs[:count]
-    keep_ref, send_ref, a_ref, h_ref, sems = refs[count:]
-    rank, wide = a_ref.shape
-    z_differs, x_differs = pos_ref[3] == 1, pos_ref[4] == 1
-    jobs = []
-    for half in range(2):
-        target = a_ref.at[half * (rank // 2) : (half + 1) * (rank // 2)]
-        late, early = (r2z_ref, rx_ref) if half == 0 else (r2x_ref, rz_ref)
-        one, two = (z_differs, x_differs) if half == 0 else (x_differs, z_differs)
-        jobs.append(
-            [
-                (one, packed_down(late, rank), target),
-                (two, packed_down(early.at[0], rank), target),
-                (None, down_at(pos_ref, down_ref, wide, half, 0, 0), target),
-            ]
-        )
+    hid = refs[6 : 6 + count]
+    keep_ref, send_ref, a_ref, h_ref = refs[6 + count :]
+    top = a_ref.shape[0] // 2
+
+    def put(half, ref):
+        a_ref[half * top : (half + 1) * top, :] = ref[0:top]
+
+    choose_late(owner_ref, *refs[:6], put)
     tokens = hid[0].shape[1]
     for i in range(count):
         for j in range(2):
             at = (2 * i + j) * tokens
             h_ref[at : at + tokens, :] = hid[i][j]
-    copy_all(jobs, sems)
     p = lax.dot_general(
         h_ref[...], a_ref[...], (((1,), (1,)), ((), ())), preferred_element_type=jnp.float32
     )
@@ -329,7 +316,7 @@
             out[j, i % far] = p[at : at + tokens]
 
 
-def attend_kernel(far, slots, meta_ref, len_ref, *refs):
+def attend_kernel(far, slots, owner_ref, len_ref, *refs):
     low = refs[:far]
     ups = refs[far : far + QUAD]
     kvs = refs[far + QUAD : far + QUAD + 3]
@@ -341,7 +328,12 @@
     query_heads = q_ref.shape[1] // HEAD_SIZE
     kv_heads = k_ref.shape[1] // HEAD_SIZE
     groups = query_heads // kv_heads
-    myself, pick = meta_ref[0], meta_ref[1]
+    _, quad, zl, x = place()
+    myself = lax.axis_index("ctx")
+    pick = (owner_ref[0] // QUAD - quad + far) % far
+    places = [(s, dz, dx) for dx in range(2) for dz in range(2) for s in range(far)]
+    ids = [((quad - s + far) % far * 2 + (zl ^ dz)) * 2 + (x ^ dx) for s, dz, dx in places]
+    blocks = [(zl ^ dz) * 2 + (x ^ dx) for dz, dx in ((0, 0), (1, 0), (0, 1), (1, 1))]
     for s in range(far):
 
         @pl.when(pick == s)
@@ -350,7 +342,7 @@
 
     lowrank = low_ref[...].astype(jnp.bfloat16)
     for i in range(QUAD):
-        d_ref[meta_ref[2 + i]] = jnp.dot(lowrank, ups[i][...], preferred_element_type=jnp.float32)
+        d_ref[blocks[i]] = jnp.dot(lowrank, ups[i][...], preferred_element_type=jnp.float32)
     pieces = [kvs[0].at[s] for s in range(far)] + [kvs[1].at[s] for s in range(far)]
     pieces += [kvs[2].at[s] for s in range(2 * far)]
     for i, piece in enumerate(pieces):
@@ -373,8 +365,8 @@
     for i in range(n):
         after = col >= i * rows
         start = jnp.where(after, i * rows, start)
-        limit = jnp.where(after, len_ref[i], limit)
-        first = jnp.where(after, meta_ref[2 + QUAD + i] * tokens, first)
+        limit = jnp.where(after, len_ref[ids[i]], limit)
+        first = jnp.where(after, ids[i] * tokens, first)
     within = col - start
     ok = jnp.where(within < slots, within - limit, within - slots + first - token - 1) < 0
     bias = jnp.where(ok, 0.0, -1e30)[None]
@@ -399,14 +391,28 @@
     return [pl.BlockSpec(memory_space=space)] * count
 
 
-def call(kernel, shapes, inputs, outputs, scratch=()):
-    return pl.pallas_call(
+def call(kernel, shapes, inputs, outputs, scratch=(), room=4 * 2**20, keep=True):
+    out_shape = [(pltpu.VMEM if keep else jax.ShapeDtypeStruct)(s, d) for s, d in shapes]
+    run = pl.pallas_call(
         kernel,
-        out_shape=[jax.ShapeDtypeStruct(s, d) for s, d in shapes],
+        out_shape=out_shape,
         in_specs=inputs,
         out_specs=outputs,
         scratch_shapes=list(scratch),
-    )
+        compiler_params=pltpu.CompilerParams(vmem_limit_bytes=room),
+    )
+
+    def placed(*args):
+        return run(
+            *(
+                pltpu.with_memory_space_constraint(a, i.memory_space)
+                if i.memory_space in (pltpu.VMEM, pltpu.HBM)
+                else a
+                for a, i in zip(args, inputs, strict=True)
+            )
+        )
+
+    return placed
 
 
 def shards_quads(
@@ -426,10 +432,9 @@
     tp_size = lax.axis_size("tp")
     far = n // QUAD
     myself = lax.axis_index("ctx")
-    core = lax.axis_index("tp")
-    quad, zl, x = myself // QUAD, myself // 2 % 2, myself % 2
+    quad = myself // QUAD
     owner = adapter_owner[0]
-    owner_quad, owner_zl, owner_x = owner // QUAD, owner // 2 % 2, owner % 2
+    owner_quad = owner // QUAD
     tokens, features = hidden.shape
     wide = features // (tp_size * QUAD)
     rank = adapter_down.shape[2]
@@ -437,7 +442,7 @@
     quarter = columns // QUAD
     slots, kv_width = stored_keys.shape
     bf16, f32 = jnp.bfloat16, jnp.float32
-    smem, vmem, anywhere = pltpu.SMEM, pltpu.VMEM, pl.ANY
+    smem, vmem, hbm = pltpu.SMEM, pltpu.VMEM, pltpu.HBM
 
     def permute(v, flip=0, shift=0, core_shift=0):
         pairs = []
@@ -448,76 +453,54 @@
         return lax.ppermute(v, ("ctx", "tp"), pairs)
 
     down, up = adapter_down[0].T, adapter_up[0]
-    pos = jnp.stack(
-        [
-            core,
-            zl,
-            x,
-            (zl != owner_zl).astype(jnp.int32),
-            (x != owner_x).astype(jnp.int32),
-        ]
-    )
-    packed = rank // 2 + rank // 4
+    packed = (rank // 2 + rank // 4, wide)
+    pair, hidden_pair = ((2, *packed), bf16), ((2, tokens, wide), bf16)
+    sems = [pltpu.SemaphoreType.DMA((14,))]
 
     sx, sz, hz = call(
-        first_kernel,
-        [((2, packed, wide), bf16), ((2, packed, wide), bf16), ((2, tokens, wide), bf16)],
-        specs(smem, 1) + specs(anywhere, 3),
-        specs(anywhere, 3),
-        [pltpu.SemaphoreType.DMA((14,))],
-    )(pos, down, up, hidden)
+        first_kernel, [pair, pair, hidden_pair], specs(hbm, 3), specs(vmem, 3), sems
+    )(down, up, hidden)
     gz = permute(hz, 2)
     rx = permute(sx, 1)
     rz = permute(sz, 2)
-
-    hx, hf = call(
-        hidden_kernel,
-        [((2, tokens, wide), bf16), ((2, tokens, wide), bf16)],
-        specs(smem, 1) + specs(anywhere, 2),
-        specs(anywhere, 2),
-        [pltpu.SemaphoreType.DMA((4,))],
-    )(pos, hidden, gz)
+    ox, oz, hh = call(
+        own_kernel, [pair, pair, hidden_pair], specs(hbm, 3), specs(vmem, 3), sems
+    )(down, up, hidden)
+
+    hx, hf = call(hidden_kernel, [hidden_pair, hidden_pair], specs(vmem, 2), specs(vmem, 2))(hh, gz)
     hg = permute(hx, 1)
     hid = [hf] + [permute(hf, 0, s) for s in range(1, far)]
     hid += [hg] + [permute(hg, 0, s) for s in range(1, far)]
 
     s2z, s2x = call(
         second_kernel,
-        [((packed, wide), bf16), ((packed, wide), bf16)],
-        specs(smem, 1) + specs(anywhere, 4),
-        specs(anywhere, 2),
-        [pltpu.SemaphoreType.DMA((6,))],
-    )(pos, down, up, rx, rz)
+        [(packed, bf16), (packed, bf16)],
+        specs(smem, 1) + specs(vmem, 4),
+        specs(vmem, 2),
+    )(adapter_owner, ox, oz, rx, rz)
     r2z = permute(s2z, 2)
     r2x = permute(s2x, 1)
+    parts = (adapter_owner, ox, oz, rx, rz, r2z, r2x)
 
     (mine,) = call(
-        up_kernel,
-        [((rank, quarter), bf16)],
-        specs(smem, 1) + specs(anywhere, 5),
-        specs(anywhere, 1),
-        [pltpu.SemaphoreType.DMA((4,))],
-    )(pos, up, rx, rz, r2z, r2x)
+        up_kernel, [((rank, quarter), bf16)], specs(smem, 1) + specs(vmem, 6), specs(vmem, 1)
+    )(*parts)
     quarters = mine
     for s in range(1, far):
         came = permute(mine, 0, s)
         quarters = jnp.where((quad - owner_quad) % far == s, came, quarters)
     up_z = permute(quarters, 2)
     up_x = permute(quarters, 1)
-    up_zx = permute(up_z, 1)
+    up_zx = permute(quarters, 3)
 
     partial_shape = ((2, far, tokens, rank), f32)
     keep, send = call(
         functools.partial(lowrank_kernel, far),
         [partial_shape, partial_shape],
-        specs(smem, 1) + specs(anywhere, 5) + specs(vmem, 2 * far),
+        specs(smem, 1) + specs(vmem, 6 + 2 * far),
         specs(vmem, 2),
-        [
-            pltpu.VMEM((rank, wide), bf16),
-            pltpu.VMEM((n * tokens, wide), bf16),
-            pltpu.SemaphoreType.DMA((2,)),
-        ],
-    )(pos, down, rx, rz, r2z, r2x, *hid)
+        [pltpu.VMEM((rank, wide), bf16), pltpu.VMEM((n * tokens, wide), bf16)],
+    )(*parts, *hid)
     total = keep
     for c in range(tp_size):
         total = total + permute(send, 1, 0, c)
@@ -527,9 +510,12 @@
     low = [total[0]] + [permute(total[s], 0, -s) for s in range(1, far)]
 
     positions = turn_start[0] + myself * tokens + jnp.arange(tokens, dtype=jnp.int32)
-    cosine, sine = rotary_tables(positions)
-    cosine = jnp.concatenate([cosine, cosine], axis=1)
-    sine = jnp.concatenate([-sine, sine], axis=1)
+    lanes = jnp.arange(HEAD_SIZE, dtype=jnp.int32)
+    place_in_half = (lanes % (HEAD_SIZE // 2)).astype(f32)
+    inverse = jnp.exp(place_in_half * (-2.0 * math.log(500000.0) / HEAD_SIZE))
+    angles = positions.astype(f32)[:, None] * inverse[None, :]
+    cosine = jnp.cos(angles)
+    sine = jnp.sin(angles) * jnp.where(lanes < HEAD_SIZE // 2, -1.0, 1.0)[None, :]
     kv_rows = 2 * (slots + tokens)
     (kv,) = call(pack_kernel, [((kv_rows, kv_width), bf16)], specs(vmem, 6), specs(vmem, 1))(
         cosine, sine, stored_keys, stored_values, unrotated_turn_keys, incoming_values
@@ -538,11 +524,6 @@
     kv_z = permute(kv, 2)
     kv_x = permute(jnp.concatenate([kv, kv_z]), 1)
 
-    places = [(s, dz, dx) for dx in range(2) for dz in range(2) for s in range(far)]
-    ids = [((quad - s) % far * 2 + (zl ^ dz)) * 2 + (x ^ dx) for s, dz, dx in places]
-    blocks = [(zl ^ dz) * 2 + (x ^ dx) for dz, dx in ((0, 0), (1, 0), (0, 1), (1, 1))]
-    meta = jnp.stack([myself, (owner_quad - quad) % far] + blocks + ids)
-    lengths = shard_lengths[jnp.stack(ids)]
     (out,) = call(
         functools.partial(attend_kernel, far, slots),
         [(q_base.shape, bf16)],
@@ -555,7 +536,9 @@
             pltpu.VMEM((n * kv_rows // 2, kv_width), bf16),
             pltpu.VMEM((tokens, rank), f32),
         ],
-    )(meta, lengths, *low, quarters, up_z, up_x, up_zx, kv, kv_z, kv_x, cosine, sine, q_base)
+        room=16 * 2**20,
+        keep=False,
+    )(adapter_owner, shard_lengths, *low, quarters, up_z, up_x, up_zx, kv, kv_z, kv_x, cosine, sine, q_base)
     return out
 
 

time: 129 us -> 63.9 us (0.50)
  Pallas kernels: 66.8 us -> 5.67 us
  local copies, waits for them, and re-layouts: 6.61 us -> 0.03 us
  waiting for transfers between devices: 26.5 us -> 30.9 us
  other arithmetic: 2.69 us -> 0.21 us
    pallas_call x7 -> x8, Pallas kernels: 66.8 us -> 5.67 us  [placed(): run(*(pltpu.with_memory_space_constraint(a, i.memory_space) if i.memory_s...]
    ppermute x20, waiting for transfers between devices: 26.5 us -> 30.9 us  [permute(): return lax.ppermute(v, ('ctx', 'tp'), pairs)]
    unnamed x38 -> x12, local copies, waits for them, and re-layouts: 3.52 us -> 0.03 us
    another operation x3 -> x0, local copies, waits for them, and re-layouts: 1.36 us -> none  [the longest x1 0.69 us: shards_quads(): meta = jnp.stack([myself, (owner_quad - quad) % far] + blocks + ids)]
  transfers between devices with their start and end apart: 20 -> 20, of which waited for: 6 -> 10; matrix products, arithmetic and copies ran while one was open for 4% -> 0% of each run, Pallas kernels for 26% -> 3%
where the time goes in v2:
time: 63.9 us; the launch traced here: 63.7 us
  waiting for transfers between devices  30.9 us (48%)
  starting transfers between devices  25.4 us (40%)
  Pallas kernels  5.67 us (9%)
  between operations  1.48 us (2%)
    ppermute x20, waiting for transfers between devices, permute(): return lax.ppermute(v, ('ctx', 'tp'), pairs)  30.9 us
    ppermute x20, starting transfers between devices, permute(): return lax.ppermute(v, ('ctx', 'tp'), pairs)  25.4 us
    pallas_call x8, Pallas kernels, placed(): run(*(pltpu.with_memory_space_constraint(a, i.memory_space) if i.memory_s...  5.67 us
  transfers between devices with their start and end apart: 20, of which 10 were waited for; matrix products, arithmetic and copies ran while one was open for 0% of the time, Pallas kernels for 3%

profile of v2, /device:TPU:0, one launch (start us, length us, event | category | flops | bytes accessed | tf_op | source)
XLA Modules:
  0.0 63.7 jit_solution(5160416263754725894)
XLA Ops:
  0.0 1.4 %shard_map.110 = (bf16[2,48,2048]{2,1,0:T(8,128)(2,1)S(1)}, bf16[2,48,2048]{2,1,0:T(8,128)(2,1)S(1)}, bf16[2,16,2048]{2,1,0:T(8,128)(2,1)S(1)}) custom-call(bf16[64,16384]{1,0:T(8,128)(2,1)} %bitcast.25, bf16[64,4096]{1,0:T(8,128)(2,1)} %bitcast.27, bf16[16,16384]{1,0:T(8,128)(2,1)} %hidden_ref.3), custom_call_target="tpu_custom_call" | custom-call | tf_op jit(solution)/shard_map/pallas_call | solution.py:406
  1.4 3.0 %collective-permute-start = (bf16[2,48,2048]{2,1,0:T(8,128)(2,1)S(1)}, bf16[2,48,2048]{2,1,0:T(8,128)(2,1)S(1)}, u32[]{:S(2)}, u32[]{:S(2)}) collective-permute-start(bf16[2,48,2048]{2,1,0:T(8,128)(2,1)S(1)} %get-tuple-element.19), channel_id=1, source_target_pairs={{0,2},{1,3},{2,0},{3,1},{4,6},{5,7},{6,4},{7,5},{8,10},{9,11},{10,... | collective-permute-start | bytes 1179656 | tf_op jit(solution)/shard_map/ppermute | solution.py:453
  4.4 1.6 %collective-permute-start.1 = (bf16[2,48,2048]{2,1,0:T(8,128)(2,1)S(1)}, bf16[2,48,2048]{2,1,0:T(8,128)(2,1)S(1)}, u32[]{:S(2)}, u32[]{:S(2)}) collective-permute-start(bf16[2,48,2048]{2,1,0:T(8,128)(2,1)S(1)} %get-tuple-element.20), channel_id=1, source_target_pairs={{0,4},{1,5},{2,6},{3,7},{4,0},{5,1},{6,2},{7,3},{8,12},{9,13},{10,... | collective-permute-start | bytes 1179656 | tf_op jit(solution)/shard_map/ppermute | solution.py:453
  6.5 1.4 %shard_map.109 = (bf16[2,48,2048]{2,1,0:T(8,128)(2,1)S(1)}, bf16[2,48,2048]{2,1,0:T(8,128)(2,1)S(1)}, bf16[2,16,2048]{2,1,0:T(8,128)(2,1)S(1)}) custom-call(bf16[64,16384]{1,0:T(8,128)(2,1)} %bitcast.26, bf16[64,4096]{1,0:T(8,128)(2,1)} %bitcast.28, bf16[16,16384]{1,0:T(8,128)(2,1)} %hidden_ref.3), custom_call_target="tpu_custom_call" | custom-call | tf_op jit(solution)/shard_map/pallas_call | solution.py:406
  8.5 9.3 %collective-permute-done.4.gz_ref = bf16[2,16,2048]{2,1,0:T(8,128)(2,1)S(1)} collective-permute-done((bf16[2,16,2048]{2,1,0:T(8,128)(2,1)S(1)}, bf16[2,16,2048]{2,1,0:T(8,128)(2,1)S(1)}, u32[]{:S(2)}, u32[]{:S(2)}) %collective-permute-start.4) | collective-permute-done | bytes 131104 | tf_op jit(solution)/shard_map/ppermute | solution.py:453
  18.9 2.8 %collective-permute-start.5 = (bf16[2,16,2048]{2,1,0:T(8,128)(2,1)S(1)}, bf16[2,16,2048]{2,1,0:T(8,128)(2,1)S(1)}, u32[]{:S(2)}, u32[]{:S(2)}) collective-permute-start(bf16[2,16,2048]{2,1,0:T(8,128)(2,1)S(1)} %get-tuple-element.25.refs_6_), channel_id=1, source_target_pairs={{0,8},{1,9},{2,10},{3,11},{4,12},{5,13},{6,14},{7,15},{8,0},{9,1},... | collective-permute-start | bytes 393224 | tf_op jit(solution)/shard_map/ppermute | solution.py:453
  21.7 1.1 %collective-permute-done.6.refs_8_ = bf16[2,16,2048]{2,1,0:T(8,128)(2,1)S(1)} collective-permute-done((bf16[2,16,2048]{2,1,0:T(8,128)(2,1)S(1)}, bf16[2,16,2048]{2,1,0:T(8,128)(2,1)S(1)}, u32[]{:S(2)}, u32[]{:S(2)}) %collective-permute-start.6) | collective-permute-done | bytes 131104 | tf_op jit(solution)/shard_map/ppermute | solution.py:453
  22.8 2.6 %collective-permute-start.7 = (bf16[2,16,2048]{2,1,0:T(8,128)(2,1)S(1)}, bf16[2,16,2048]{2,1,0:T(8,128)(2,1)S(1)}, u32[]{:S(2)}, u32[]{:S(2)}) collective-permute-start(bf16[2,16,2048]{2,1,0:T(8,128)(2,1)S(1)} %collective-permute-done.6.refs_8_), channel_id=1, source_target_pairs={{0,8},{1,9},{2,10},{3,11},{4,12},{5,13},{6,14},{7,15},{8,0},{9,1},... | collective-permute-start | bytes 393224 | tf_op jit(solution)/shard_map/ppermute | solution.py:453
  25.5 1.6 %collective-permute-start.2 = (bf16[48,2048]{1,0:T(8,128)(2,1)S(1)}, bf16[48,2048]{1,0:T(8,128)(2,1)S(1)}, u32[]{:S(2)}, u32[]{:S(2)}) collective-permute-start(bf16[48,2048]{1,0:T(8,128)(2,1)S(1)} %get-tuple-element.21), channel_id=1, source_target_pairs={{0,4},{1,5},{2,6},{3,7},{4,0},{5,1},{6,2},{7,3},{8,12},{9,13},{10,... | collective-permute-start | bytes 589832 | tf_op jit(solution)/shard_map/ppermute | solution.py:453
  28.2 1.8 %collective-permute-done.5.refs_7_ = bf16[2,16,2048]{2,1,0:T(8,128)(2,1)S(1)} collective-permute-done((bf16[2,16,2048]{2,1,0:T(8,128)(2,1)S(1)}, bf16[2,16,2048]{2,1,0:T(8,128)(2,1)S(1)}, u32[]{:S(2)}, u32[]{:S(2)}) %collective-permute-start.5) | collective-permute-done | bytes 131104 | tf_op jit(solution)/shard_map/ppermute | solution.py:453
  30.0 5.0 %collective-permute-done.7.refs_9_ = bf16[2,16,2048]{2,1,0:T(8,128)(2,1)S(1)} collective-permute-done((bf16[2,16,2048]{2,1,0:T(8,128)(2,1)S(1)}, bf16[2,16,2048]{2,1,0:T(8,128)(2,1)S(1)}, u32[]{:S(2)}, u32[]{:S(2)}) %collective-permute-start.7) | collective-permute-done | bytes 131104 | tf_op jit(solution)/shard_map/ppermute | solution.py:453
  35.5 1.5 %collective-permute-start.8 = (f32[2,2,16,64]{3,2,1,0:T(8,128)S(1)}, f32[2,2,16,64]{3,2,1,0:T(8,128)S(1)}, u32[]{:S(2)}, u32[]{:S(2)}) collective-permute-start(f32[2,2,16,64]{3,2,1,0:T(8,128)S(1)} %get-tuple-element.28), channel_id=1, source_target_pairs={{0,2},{1,3},{2,0},{3,1},{4,6},{5,7},{6,4},{7,5},{8,10},{9,11},{10,... | collective-permute-start | bytes 49160 | tf_op jit(solution)/shard_map/ppermute | solution.py:453
  37.3 0.6 collective-permute-start.18
  38.2 0.9 %collective-permute-done.9 = f32[2,2,16,64]{3,2,1,0:T(8,128)S(1)} collective-permute-done((f32[2,2,16,64]{3,2,1,0:T(8,128)S(1)}, f32[2,2,16,64]{3,2,1,0:T(8,128)S(1)}, u32[]{:S(2)}, u32[]{:S(2)}) %collective-permute-start.9) | collective-permute-done | bytes 16416 | tf_op jit(solution)/shard_map/ppermute | solution.py:453
  39.5 0.8 %collective-permute-start.11 = (f32[2,16,64]{2,1,0:T(8,128)S(1)}, f32[2,16,64]{2,1,0:T(8,128)S(1)}, u32[]{:S(2)}, u32[]{:S(2)}) collective-permute-start(f32[2,16,64]{2,1,0:T(8,128)S(1)} %slice_bitcast_fusion), channel_id=1, source_target_pairs={{0,4},{1,5},{2,6},{3,7},{4,0},{5,1},{6,2},{7,3},{8,12},{9,13},{10,... | collective-permute-start | bytes 24584 | tf_op jit(solution)/shard_map/ppermute | solution.py:453
  40.3 3.5 %collective-permute-done.18.refs_7_ = bf16[2,160,256]{2,1,0:T(8,128)(2,1)S(1)} collective-permute-done((bf16[2,160,256]{2,1,0:T(8,128)(2,1)S(1)}, bf16[2,160,256]{2,1,0:T(8,128)(2,1)S(1)}, u32[]{:S(2)}, u32[]{:S(2)}) %collective-permute-start.18) | collective-permute-done | bytes 163872 | tf_op jit(solution)/shard_map/ppermute | solution.py:453
  43.8 1.3 %collective-permute-start.19 = (bf16[4,160,256]{2,1,0:T(8,128)(2,1)S(1)}, bf16[4,160,256]{2,1,0:T(8,128)(2,1)S(1)}, u32[]{:S(2)}, u32[]{:S(2)}) collective-permute-start(bf16[4,160,256]{2,1,0:T(8,128)(2,1)S(1)} %pad_maximum_fusion), channel_id=1, source_target_pairs={{0,2},{1,3},{2,0},{3,1},{4,6},{5,7},{6,4},{7,5},{8,10},{9,11},{10,... | collective-permute-start | bytes 983048 | tf_op jit(solution)/shard_map/ppermute | solution.py:453
  45.2 2.0 %collective-permute-start.13 = (bf16[64,1024]{1,0:T(8,128)(2,1)S(1)}, bf16[64,1024]{1,0:T(8,128)(2,1)S(1)}, u32[]{:S(2)}, u32[]{:S(2)}) collective-permute-start(bf16[64,1024]{1,0:T(8,128)(2,1)S(1)} %shard_map.114), channel_id=1, source_target_pairs={{0,8},{1,9},{2,10},{3,11},{4,12},{5,13},{6,14},{7,15},{8,0},{9,1},... | collective-permute-start | bytes 393224 | tf_op jit(solution)/shard_map/ppermute | solution.py:453
  47.2 5.9 %collective-permute-done.13 = bf16[64,1024]{1,0:T(8,128)(2,1)S(1)} collective-permute-done((bf16[64,1024]{1,0:T(8,128)(2,1)S(1)}, bf16[64,1024]{1,0:T(8,128)(2,1)S(1)}, u32[]{:S(2)}, u32[]{:S(2)}) %collective-permute-start.13) | collective-permute-done | bytes 131104 | tf_op jit(solution)/shard_map/ppermute | solution.py:453
  53.4 1.0 %collective-permute-start.15 = (bf16[64,1024]{1,0:T(8,128)(2,1)S(1)}, bf16[64,1024]{1,0:T(8,128)(2,1)S(1)}, u32[]{:S(2)}, u32[]{:S(2)}) collective-permute-start(bf16[64,1024]{1,0:T(8,128)(2,1)S(1)} %broadcast_select_fusion.refs_2_), channel_id=1, source_target_pairs={{0,2},{1,3},{2,0},{3,1},{4,6},{5,7},{6,4},{7,5},{8,10},{9,11},{10,... | collective-permute-start | bytes 393224 | tf_op jit(solution)/shard_map/ppermute | solution.py:453
  54.3 2.3 %collective-permute-start.16 = (bf16[64,1024]{1,0:T(8,128)(2,1)S(1)}, bf16[64,1024]{1,0:T(8,128)(2,1)S(1)}, u32[]{:S(2)}, u32[]{:S(2)}) collective-permute-start(bf16[64,1024]{1,0:T(8,128)(2,1)S(1)} %broadcast_select_fusion.refs_2_), channel_id=1, source_target_pairs={{0,6},{1,7},{2,4},{3,5},{4,2},{5,3},{6,0},{7,1},{8,14},{9,15},{10,... | collective-permute-start | bytes 393224 | tf_op jit(solution)/shard_map/ppermute | solution.py:453
  56.6 1.7 %collective-permute-start.12 = (f32[16,64]{1,0:T(8,128)S(1)}, f32[16,64]{1,0:T(8,128)S(1)}, u32[]{:S(2)}, u32[]{:S(2)}) collective-permute-start(f32[16,64]{1,0:T(8,128)S(1)} %get-tuple-element.29), channel_id=1, source_target_pairs={{0,8},{1,9},{2,10},{3,11},{4,12},{5,13},{6,14},{7,15},{8,0},{9,1},... | collective-permute-start | bytes 12296 | tf_op jit(solution)/shard_map/ppermute | solution.py:453
  58.3 2.9 %collective-permute-done.12.refs_1_ = f32[16,64]{1,0:T(8,128)S(1)} collective-permute-done((f32[16,64]{1,0:T(8,128)S(1)}, f32[16,64]{1,0:T(8,128)S(1)}, u32[]{:S(2)}, u32[]{:S(2)}) %collective-permute-start.12) | collective-permute-done | bytes 4128 | tf_op jit(solution)/shard_map/ppermute | solution.py:453
  61.2 2.5 %shard_map.116 = bf16[16,4096]{1,0:T(8,128)(2,1)} custom-call(s32[1]{0:T(128)} %copy.12.owner_ref, s32[8]{0:T(128)S(1)} %copy-done.5, f32[16,64]{1,0:T(8,128)S(1)} %get-tuple-element.30.refs_0_, f32[16,64]{1,0:T(8,128)S(1)} %collective-permute-done.12.refs_1_, bf16[64,1024]{1,0:T(8,128)(2,1)S(1)} %broadcast_select_fusion.refs_2_, ...), custom_call_target="tpu_custom_call" | custom-call | tf_op jit(solution)/shard_map/pallas_call | solution.py:406
  (46 shorter events, 3.9 us)
Async XLA Ops:
  1.4 24.1 %collective-permute-start = (bf16[2,48,2048]{2,1,0:T(8,128)(2,1)S(1)}, bf16[2,48,2048]{2,1,0:T(8,128)(2,1)S(1)}, u32[]{:S(2)}, u32[]{:S(2)}) collective-permute-start(bf16[2,48,2048]{2,1,0:T(8,128)(2,1)S(1)} %get-tuple-element.19), channel_id=1, source_target_pairs={{0,2},{1,3},{2,0},{3,1},{4,6},{5,7},{6,4},{7,5},{8,10},{9,11},{10,... | collective-permute-start | bytes 1179656 | tf_op jit(solution)/shard_map/ppermute | solution.py:453
  4.4 21.0 %collective-permute-start.1 = (bf16[2,48,2048]{2,1,0:T(8,128)(2,1)S(1)}, bf16[2,48,2048]{2,1,0:T(8,128)(2,1)S(1)}, u32[]{:S(2)}, u32[]{:S(2)}) collective-permute-start(bf16[2,48,2048]{2,1,0:T(8,128)(2,1)S(1)} %get-tuple-element.20), channel_id=1, source_target_pairs={{0,4},{1,5},{2,6},{3,7},{4,0},{5,1},{6,2},{7,3},{8,12},{9,13},{10,... | collective-permute-start | bytes 1179656 | tf_op jit(solution)/shard_map/ppermute | solution.py:453
  6.0 21.8 %copy-start.3 = (bf16[16,256]{1,0:T(8,128)(2,1)S(1)}, bf16[16,256]{1,0:T(8,128)(2,1)}, u32[]{:S(2)}) copy-start(bf16[16,256]{1,0:T(8,128)(2,1)} %tk_ref.1) | copy-start | bytes 24580
  6.0 21.8 %copy-start.4 = (bf16[16,256]{1,0:T(8,128)(2,1)S(1)}, bf16[16,256]{1,0:T(8,128)(2,1)}, u32[]{:S(2)}) copy-start(bf16[16,256]{1,0:T(8,128)(2,1)} %tv_ref.1) | copy-start | bytes 24580
  6.0 11.8 %collective-permute-start.4 = (bf16[2,16,2048]{2,1,0:T(8,128)(2,1)S(1)}, bf16[2,16,2048]{2,1,0:T(8,128)(2,1)S(1)}, u32[]{:S(2)}, u32[]{:S(2)}) collective-permute-start(bf16[2,16,2048]{2,1,0:T(8,128)(2,1)S(1)} %get-tuple-element.24), channel_id=1, source_target_pairs={{0,4},{1,5},{2,6},{3,7},{4,0},{5,1},{6,2},{7,3},{8,12},{9,13},{10,... | collective-permute-start | bytes 393224 | tf_op jit(solution)/shard_map/ppermute | solution.py:453
  17.8 5.0 %collective-permute-start.6 = (bf16[2,16,2048]{2,1,0:T(8,128)(2,1)S(1)}, bf16[2,16,2048]{2,1,0:T(8,128)(2,1)S(1)}, u32[]{:S(2)}, u32[]{:S(2)}) collective-permute-start(bf16[2,16,2048]{2,1,0:T(8,128)(2,1)S(1)} %get-tuple-element.26), channel_id=1, source_target_pairs={{0,2},{1,3},{2,0},{3,1},{4,6},{5,7},{6,4},{7,5},{8,10},{9,11},{10,... | collective-permute-start | bytes 393224 | tf_op jit(solution)/shard_map/ppermute | solution.py:453
  18.9 11.1 %collective-permute-start.5 = (bf16[2,16,2048]{2,1,0:T(8,128)(2,1)S(1)}, bf16[2,16,2048]{2,1,0:T(8,128)(2,1)S(1)}, u32[]{:S(2)}, u32[]{:S(2)}) collective-permute-start(bf16[2,16,2048]{2,1,0:T(8,128)(2,1)S(1)} %get-tuple-element.25.refs_6_), channel_id=1, source_target_pairs={{0,8},{1,9},{2,10},{3,11},{4,12},{5,13},{6,14},{7,15},{8,0},{9,1},... | collective-permute-start | bytes 393224 | tf_op jit(solution)/shard_map/ppermute | solution.py:453
  22.8 12.2 %collective-permute-start.7 = (bf16[2,16,2048]{2,1,0:T(8,128)(2,1)S(1)}, bf16[2,16,2048]{2,1,0:T(8,128)(2,1)S(1)}, u32[]{:S(2)}, u32[]{:S(2)}) collective-permute-start(bf16[2,16,2048]{2,1,0:T(8,128)(2,1)S(1)} %collective-permute-done.6.refs_8_), channel_id=1, source_target_pairs={{0,8},{1,9},{2,10},{3,11},{4,12},{5,13},{6,14},{7,15},{8,0},{9,1},... | collective-permute-start | bytes 393224 | tf_op jit(solution)/shard_map/ppermute | solution.py:453
  25.5 9.6 %collective-permute-start.2 = (bf16[48,2048]{1,0:T(8,128)(2,1)S(1)}, bf16[48,2048]{1,0:T(8,128)(2,1)S(1)}, u32[]{:S(2)}, u32[]{:S(2)}) collective-permute-start(bf16[48,2048]{1,0:T(8,128)(2,1)S(1)} %get-tuple-element.21), channel_id=1, source_target_pairs={{0,4},{1,5},{2,6},{3,7},{4,0},{5,1},{6,2},{7,3},{8,12},{9,13},{10,... | collective-permute-start | bytes 589832 | tf_op jit(solution)/shard_map/ppermute | solution.py:453
  27.1 7.9 %collective-permute-start.3 = (bf16[48,2048]{1,0:T(8,128)(2,1)S(1)}, bf16[48,2048]{1,0:T(8,128)(2,1)S(1)}, u32[]{:S(2)}, u32[]{:S(2)}) collective-permute-start(bf16[48,2048]{1,0:T(8,128)(2,1)S(1)} %get-tuple-element.22), channel_id=1, source_target_pairs={{0,2},{1,3},{2,0},{3,1},{4,6},{5,7},{6,4},{7,5},{8,10},{9,11},{10,... | collective-permute-start | bytes 589832 | tf_op jit(solution)/shard_map/ppermute | solution.py:453
  27.9 9.4 %collective-permute-start.17 = (bf16[160,256]{1,0:T(8,128)(2,1)S(1)}, bf16[160,256]{1,0:T(8,128)(2,1)S(1)}, u32[]{:S(2)}, u32[]{:S(2)}) collective-permute-start(bf16[160,256]{1,0:T(8,128)(2,1)S(1)} %shard_map.115), channel_id=1, source_target_pairs={{0,8},{1,9},{2,10},{3,11},{4,12},{5,13},{6,14},{7,15},{8,0},{9,1},... | collective-permute-start | bytes 245768 | tf_op jit(solution)/shard_map/ppermute | solution.py:453
  35.4 25.8 %copy-start = (bf16[16,4096]{1,0:T(8,128)(2,1)S(1)}, bf16[16,4096]{1,0:T(8,128)(2,1)}, u32[]{:S(2)}) copy-start(bf16[16,4096]{1,0:T(8,128)(2,1)} %refs_11_.1) | copy-start | bytes 393220
  35.4 25.8 %copy-start.5 = (s32[8]{0:T(128)S(1)}, s32[8]{0:T(128)}, u32[]{:S(2)}) copy-start(s32[8]{0:T(128)} %len_ref.1) | copy-start | bytes 100
  35.4 3.7 %collective-permute-start.9 = (f32[2,2,16,64]{3,2,1,0:T(8,128)S(1)}, f32[2,2,16,64]{3,2,1,0:T(8,128)S(1)}, u32[]{:S(2)}, u32[]{:S(2)}) collective-permute-start(f32[2,2,16,64]{3,2,1,0:T(8,128)S(1)} %get-tuple-element.28), channel_id=1, source_target_pairs={{0,3},{1,2},{2,1},{3,0},{4,7},{5,6},{6,5},{7,4},{8,11},{9,10},{10,... | collective-permute-start | bytes 49160 | tf_op jit(solution)/shard_map/ppermute | solution.py:453
  35.5 4.0 %collective-permute-start.8 = (f32[2,2,16,64]{3,2,1,0:T(8,128)S(1)}, f32[2,2,16,64]{3,2,1,0:T(8,128)S(1)}, u32[]{:S(2)}, u32[]{:S(2)}) collective-permute-start(f32[2,2,16,64]{3,2,1,0:T(8,128)S(1)} %get-tuple-element.28), channel_id=1, source_target_pairs={{0,2},{1,3},{2,0},{3,1},{4,6},{5,7},{6,4},{7,5},{8,10},{9,11},{10,... | collective-permute-start | bytes 49160 | tf_op jit(solution)/shard_map/ppermute | solution.py:453
  36.9 1.3 %collective-permute-start.10 = (f32[2,2,16,64]{3,2,1,0:T(8,128)S(1)}, f32[2,2,16,64]{3,2,1,0:T(8,128)S(1)}, u32[]{:S(2)}, u32[]{:S(2)}) collective-permute-start(f32[2,2,16,64]{3,2,1,0:T(8,128)S(1)} %get-tuple-element.27), channel_id=1, source_target_pairs={{0,1},{1,0},{2,3},{3,2},{4,5},{5,4},{6,7},{7,6},{8,9},{9,8},{10,11... | collective-permute-start | bytes 49160 | tf_op jit(solution)/shard_map/ppermute | solution.py:453
  37.3 6.5 %collective-permute-start.18 = (bf16[2,160,256]{2,1,0:T(8,128)(2,1)S(1)}, bf16[2,160,256]{2,1,0:T(8,128)(2,1)S(1)}, u32[]{:S(2)}, u32[]{:S(2)}) collective-permute-start(bf16[2,160,256]{2,1,0:T(8,128)(2,1)S(1)} %pad_maximum_fusion.1.refs_6_), channel_id=1, source_target_pairs={{0,4},{1,5},{2,6},{3,7},{4,0},{5,1},{6,2},{7,3},{8,12},{9,13},{10,... | collective-permute-start | bytes 491528 | tf_op jit(solution)/shard_map/ppermute | solution.py:453
  39.5 7.7 %collective-permute-start.11 = (f32[2,16,64]{2,1,0:T(8,128)S(1)}, f32[2,16,64]{2,1,0:T(8,128)S(1)}, u32[]{:S(2)}, u32[]{:S(2)}) collective-permute-start(f32[2,16,64]{2,1,0:T(8,128)S(1)} %slice_bitcast_fusion), channel_id=1, source_target_pairs={{0,4},{1,5},{2,6},{3,7},{4,0},{5,1},{6,2},{7,3},{8,12},{9,13},{10,... | collective-permute-start | bytes 24584 | tf_op jit(solution)/shard_map/ppermute | solution.py:453
  43.8 14.5 %collective-permute-start.19 = (bf16[4,160,256]{2,1,0:T(8,128)(2,1)S(1)}, bf16[4,160,256]{2,1,0:T(8,128)(2,1)S(1)}, u32[]{:S(2)}, u32[]{:S(2)}) collective-permute-start(bf16[4,160,256]{2,1,0:T(8,128)(2,1)S(1)} %pad_maximum_fusion), channel_id=1, source_target_pairs={{0,2},{1,3},{2,0},{3,1},{4,6},{5,7},{6,4},{7,5},{8,10},{9,11},{10,... | collective-permute-start | bytes 983048 | tf_op jit(solution)/shard_map/ppermute | solution.py:453
  45.2 7.9 %collective-permute-start.13 = (bf16[64,1024]{1,0:T(8,128)(2,1)S(1)}, bf16[64,1024]{1,0:T(8,128)(2,1)S(1)}, u32[]{:S(2)}, u32[]{:S(2)}) collective-permute-start(bf16[64,1024]{1,0:T(8,128)(2,1)S(1)} %shard_map.114), channel_id=1, source_target_pairs={{0,8},{1,9},{2,10},{3,11},{4,12},{5,13},{6,14},{7,15},{8,0},{9,1},... | collective-permute-start | bytes 393224 | tf_op jit(solution)/shard_map/ppermute | solution.py:453
  53.1 8.1 %collective-permute-start.14 = (bf16[64,1024]{1,0:T(8,128)(2,1)S(1)}, bf16[64,1024]{1,0:T(8,128)(2,1)S(1)}, u32[]{:S(2)}, u32[]{:S(2)}) collective-permute-start(bf16[64,1024]{1,0:T(8,128)(2,1)S(1)} %broadcast_select_fusion.refs_2_), channel_id=1, source_target_pairs={{0,4},{1,5},{2,6},{3,7},{4,0},{5,1},{6,2},{7,3},{8,12},{9,13},{10,... | collective-permute-start | bytes 393224 | tf_op jit(solution)/shard_map/ppermute | solution.py:453
  53.4 7.8 %collective-permute-start.15 = (bf16[64,1024]{1,0:T(8,128)(2,1)S(1)}, bf16[64,1024]{1,0:T(8,128)(2,1)S(1)}, u32[]{:S(2)}, u32[]{:S(2)}) collective-permute-start(bf16[64,1024]{1,0:T(8,128)(2,1)S(1)} %broadcast_select_fusion.refs_2_), channel_id=1, source_target_pairs={{0,2},{1,3},{2,0},{3,1},{4,6},{5,7},{6,4},{7,5},{8,10},{9,11},{10,... | collective-permute-start | bytes 393224 | tf_op jit(solution)/shard_map/ppermute | solution.py:453
  54.3 6.8 %collective-permute-start.16 = (bf16[64,1024]{1,0:T(8,128)(2,1)S(1)}, bf16[64,1024]{1,0:T(8,128)(2,1)S(1)}, u32[]{:S(2)}, u32[]{:S(2)}) collective-permute-start(bf16[64,1024]{1,0:T(8,128)(2,1)S(1)} %broadcast_select_fusion.refs_2_), channel_id=1, source_target_pairs={{0,6},{1,7},{2,4},{3,5},{4,2},{5,3},{6,0},{7,1},{8,14},{9,15},{10,... | collective-permute-start | bytes 393224 | tf_op jit(solution)/shard_map/ppermute | solution.py:453
  56.6 4.5 %collective-permute-start.12 = (f32[16,64]{1,0:T(8,128)S(1)}, f32[16,64]{1,0:T(8,128)S(1)}, u32[]{:S(2)}, u32[]{:S(2)}) collective-permute-start(f32[16,64]{1,0:T(8,128)S(1)} %get-tuple-element.29), channel_id=1, source_target_pairs={{0,8},{1,9},{2,10},{3,11},{4,12},{5,13},{6,14},{7,15},{8,0},{9,1},... | collective-permute-start | bytes 12296 | tf_op jit(solution)/shard_map/ppermute | solution.py:453
  (2 other events, 43.6 us)
